TPU v7x, 32 devices: a whole 2x2x4 slice. The times are simulated.
32 devices in a mesh: rep: 8 (over y, x, core), shard: 4 (over z).
Axes of the slice: x: 2, y: 2, z: 4, core: 2. Of those that a mesh axis runs over, the one named last changes fastest.
Arguments:
- hidden_in: bfloat16 [16384, 960], P(('rep', 'shard')), may hold values from -6 to 6
- cotangent: bfloat16 [16384, 960], P(('rep', 'shard')), may hold values from -6 to 6
- destination: int32 [16384], P(('rep', 'shard')), may hold values from 0 to 16383, as said below
- seq_lengths: int32 [4, 8], P('shard'), may hold values from 1 to 3584, 3840 in all within a row
- gate_mask: int32 [16384], P(('rep', 'shard')), may hold values 0 or 1
- query_weight: bfloat16 [960, 960], P('shard'), may hold values from -0.1875 to 0.1875
- key_matrix: bfloat16 [960, 320], P('shard'), may hold values from -0.1875 to 0.1875
- value_matrix: bfloat16 [960, 320], P('shard'), may hold values from -0.1875 to 0.1875
- out_weight: bfloat16 [960, 960], P('shard'), may hold values from -0.75 to 0.75
- gate_weight: bfloat16 [960, 2560], P('shard'), may hold values from -0.1875 to 0.1875
- up_weight: bfloat16 [960, 2560], P('shard'), may hold values from -0.1875 to 0.1875
- down_weight: bfloat16 [2560, 960], P('shard'), may hold values from -0.125 to 0.125
- attn_gain: bfloat16 [960], P('shard'), may hold values from 0.099609375 to 1.8984375
- ffn_gain: bfloat16 [960], P('shard'), may hold values from 0.099609375 to 1.8984375
- router_weight: bfloat16 [960], P('shard'), may hold values from -0.1875 to 0.1875
Outputs:
- outputs: bfloat16 [16384, 960], P(('rep', 'shard'))
- hidden_grad: bfloat16 [16384, 960], P(('rep', 'shard'))
- query_weight_grad: float32 [960, 960], P('shard')
- key_weight_grad: float32 [960, 320], P('shard')
- value_weight_grad: float32 [960, 320], P('shard')
- out_weight_grad: float32 [960, 960], P('shard')
- gate_weight_grad: float32 [960, 2560], P('shard')
- up_weight_grad: float32 [960, 2560], P('shard')
- down_weight_grad: float32 [2560, 960], P('shard')
- attn_gain_grad: float32 [960], P('shard')
- ffn_gain_grad: float32 [960], P('shard')
- router_weight_grad: float32 [960], P('shard')
Inputs may be any that keep to these rules, and one draw needn't show every extreme that they name: Each balanced position is the destination of exactly one token, and each device's 512 initial tokens go exactly 16 to each device's block of 512 balanced positions. `seq_lengths`: each line's lengths sum to 3840; the line's last 256 places are padding; the longest is 3584.
All inputs are finite; a program needn't handle non-finite values. No bound on the sum of `gate_mask` on one device may be relied on, other than what follows from the above.
Results may differ from a plain program's by a relative error of at most 0.023.
Values may be sent and summed in bfloat16 or wider, within the bound.
A program may use at most 192 MiB of HBM per device.

v0:
```python
import functools
import types

import jax
import jax.numpy as jnp
from jax import lax
from jax.experimental import pallas as pl
from jax.experimental.pallas import tpu as pltpu
from jax.sharding import Mesh
from jax.sharding import PartitionSpec as P

QUERY_HEADS = 15
KEY_VALUE_HEADS = 5
HEAD_DIM = 64
GROUP = QUERY_HEADS // KEY_VALUE_HEADS
EPSILON = 1e-05
NEGATIVE_HUGE = -1e30
ROPE_BASE = 10000.0
FF_CHUNK = 256
bf16 = jnp.bfloat16
f32 = jnp.float32
MESH = pl.DeviceIdType.MESH
REP = ("chip", "core")
ALL = ("chip", "core", "shard")
VMEM_SPEC = pl.BlockSpec(memory_space=pltpu.VMEM)
HBM_SPEC = pl.BlockSpec(memory_space=pl.ANY)


def dot(a, b, ca=1, cb=0):
    return lax.dot_general(a, b, (((ca,), (cb,)), ((), ())), preferred_element_type=f32)


def axes_size(sizes, axes):
    total = 1
    for name in axes:
        total *= sizes[name]
    return total


def peer_coords(index, axes, sizes):
    coords = {}
    for name in reversed(axes):
        coords[name] = lax.rem(index, sizes[name])
        index = index // sizes[name]
    return coords


def partner(k, axes, sizes, back=False):
    if axes == ALL:
        reps = axes_size(sizes, REP)
        offsets = {"chip": lax.rem(k, reps) // 2, "core": lax.rem(k, 2), "shard": k // reps}
    elif axes == REP:
        offsets = {"chip": k // 2, "core": lax.rem(k, 2)}
    else:
        offsets = {axes[0]: k}
    coords, index = {}, 0
    for name in axes:
        me, count, offset = lax.axis_index(name), sizes[name], offsets[name]
        if name == "chip" and count == 4:
            x = lax.rem(lax.rem(me, 2) + lax.rem(offset, 2), 2)
            coords[name] = 2 * lax.rem(me // 2 + offset // 2, 2) + x
        else:
            coords[name] = lax.rem(me + (count - offset if back else offset), count)
        index = index * count + coords[name]
    return index, coords


def remote(src, dst, send_sem, recv_sem, coords):
    return pltpu.make_async_remote_copy(
        src_ref=src,
        dst_ref=dst,
        send_sem=send_sem,
        recv_sem=recv_sem,
        device_id=coords,
        device_id_type=MESH,
    )


def each(start, stop, body):
    def step(k, carry):
        body(k)
        return carry

    lax.fori_loop(start, stop, step, 0)


class Item:
    late = False
    final = False
    aliased = False
    pre = 0
    hooks = ()

    def at(self, *hooks):
        self.hooks = hooks
        return self

    def steps(self, ins, outs, scratch):
        yield


class AllToAll(Item):
    final = True

    def __init__(self, sizes, array, axes, spread=False, by_shard=False, late=False, source=None):
        self.sizes, self.axes, self.spread, self.late = sizes, axes, spread, late
        self.by_shard = by_shard
        self.count = axes_size(sizes, axes)
        self.source = source
        self.inputs = [] if source is not None else [array]
        piece = tuple(array.shape) if spread else tuple(array.shape[1:])
        self.in_specs = [VMEM_SPEC] * len(self.inputs)
        self.out_shapes = [jax.ShapeDtypeStruct((self.count,) + piece, array.dtype)]
        self.out_specs = [VMEM_SPEC]
        self.scratch = [
            pltpu.SemaphoreType.DMA((self.count,)),
            pltpu.SemaphoreType.DMA((self.count,)),
        ]

    def index(self, peer):
        return lax.rem(peer, self.sizes["shard"]) if self.by_shard else peer

    def copy(self, k, ins, outs, scratch):
        me = lax.axis_index(self.axes)
        peer, coords = partner(k, self.axes, self.sizes)
        return remote(
            ins[0] if self.spread else ins[0].at[self.index(peer)],
            outs[0].at[me],
            scratch[0].at[k],
            scratch[1].at[k],
            coords,
        )

    def steps(self, ins, outs, scratch):
        each(1, self.count, lambda k: self.copy(k, ins, outs, scratch).start())
        me = lax.axis_index(self.axes)
        outs[0][me] = ins[0][...] if self.spread else ins[0][self.index(me)]
        yield
        each(1, self.count, lambda k: self.copy(k, ins, outs, scratch).wait())


class Swap(AllToAll):
    def __init__(self, sizes, array):
        super().__init__(sizes, array, ("core",), spread=True, late=True)
        self.inputs, self.in_specs = [], []

    def steps(self, ins, outs, scratch):
        core = lax.axis_index("core")

        def copy():
            here = outs[0].at[core]
            return remote(here, here, scratch[0].at[1], scratch[1].at[1], {"core": 1 - core})

        copy().start()
        yield
        copy().wait()


class Stepwise(AllToAll):
    def __init__(self, sizes, array, source):
        super().__init__(sizes, array, REP, source=source)

    def copy_to(self, peer):
        me = lax.axis_index(REP)
        return remote(
            self.src.at[peer],
            self.dst.at[me],
            self.sems[0].at[peer],
            self.sems[1].at[me],
            peer_coords(peer, REP, self.sizes),
        )

    def send(self, peer):
        pl.when(peer != lax.axis_index(REP))(lambda: self.copy_to(peer).start())

    def steps(self, ins, outs, scratch):
        self.src, self.dst, self.sems = ins[0], outs[0], scratch
        yield
        me = lax.axis_index(REP)
        outs[0][me] = ins[0][me]

        def wait(k):
            peer = lax.rem(me + k, self.count)
            remote(
                self.src.at[me],
                self.dst.at[peer],
                self.sems[0].at[peer],
                self.sems[1].at[peer],
                peer_coords(peer, REP, self.sizes),
            ).wait_recv()
            self.copy_to(peer).wait_send()

        each(1, self.count, wait)


class Heads(Item):
    final = True
    late = True

    def __init__(self, sizes, array, to, source):
        self.sizes, self.to, self.source = sizes, to, source
        self.count = axes_size(sizes, REP)
        self.slots = array.shape[1] // 3
        self.main = array.shape[1] if self.slots != 2 else 4
        self.units = array.shape[1]
        self.inputs, self.in_specs = [], []
        self.out_shapes = [jax.ShapeDtypeStruct(array.shape, array.dtype)]
        self.out_specs = [VMEM_SPEC]
        dma = pltpu.SemaphoreType.DMA
        self.scratch = [dma((2, self.count)), dma((2, self.count))]

    def copy(self, k, ins, outs, scratch, extra, sending):
        me = lax.axis_index(REP)
        peer, coords = partner(k, REP, self.sizes, not sending)
        units = pl.ds(self.main, self.units - self.main) if extra else pl.ds(0, self.main)
        return peer, remote(
            ins[0].at[peer, units],
            outs[0].at[me if sending else peer, units],
            scratch[0].at[int(extra), k],
            scratch[1].at[int(extra), k],
            coords,
        )

    def every(self, ins, outs, scratch, sending, act):
        def main(k):
            act(self.copy(k, ins, outs, scratch, False, sending)[1])

        def extra(k):
            peer, copy = self.copy(k, ins, outs, scratch, True, sending)
            owner = peer if sending == self.to else lax.axis_index(REP)
            pl.when(apart(owner) == 1)(lambda: act(copy))

        each(1, self.count, main)
        if self.units > self.main:
            each(1, self.count, extra)

    def steps(self, ins, outs, scratch):
        self.every(ins, outs, scratch, True, lambda copy: copy.start())
        me = lax.axis_index(REP)
        outs[0][me] = ins[0][me]
        yield
        self.every(ins, outs, scratch, False, lambda copy: copy.wait_recv())
        self.every(ins, outs, scratch, True, lambda copy: copy.wait_send())


def apart(rep):
    last = KEY_VALUE_HEADS - 1
    return jnp.minimum((2 * rep + 1) // GROUP, last) - jnp.minimum((2 * rep) // GROUP, last)


def key_slots(slots):
    return [0, apart(lax.axis_index(REP))] if slots == 2 else list(range(slots))


def key_unit(slots, slot):
    return slots + 2 * slot


def value_unit(slots, slot):
    return slots + 2 * slot + 1


def flipped(chip, k):
    x, y = lax.rem(chip, 2), chip // 2
    x = 1 - x if k in (1, 3) else x
    y = 1 - y if k in (2, 3) else y
    return 2 * y + x


class Plane:
    def __init__(self, sizes, pair, lo, hi):
        self.pair, self.lo, self.hi, self.chips = pair, lo, hi, sizes["chip"]
        self.relay = self.chips == 4
        self.near = (1, 2) if self.relay else tuple(range(1, self.chips))
        self.scratch = [pltpu.SemaphoreType.DMA((self.chips, hi))] * (4 if pair else 2)

    def bind(self, region, path, guard, other, sems):
        self.region, self.path, self.guard, self.other, self.sems = region, path, guard, other, sems
        self.chip, self.core = lax.axis_index("chip"), lax.axis_index("core")

    def peer(self, k):
        return flipped(self.chip, k) if self.relay else lax.rem(self.chip + k, self.chips)

    def owner(self, k):
        if self.relay:
            return flipped(self.chip, k)
        return lax.rem(self.chip + self.chips - k, self.chips)

    def copy(self, t, k, owner, to):
        ref = self.region(t, owner, self.core)
        return remote(ref, ref, self.sems[0].at[k, t], self.sems[1].at[k, t], {"chip": to})

    def relayed(self, t, k):
        return self.copy(t, 3, self.owner(k), self.peer(3 - k))

    def pass_on(self, t, owner, core=None):
        ref = self.region(t, owner, self.core if core is None else core)
        return remote(
            ref, ref, self.sems[2].at[owner, t], self.sems[3].at[owner, t], {"core": 1 - self.core}
        )

    def parts(self, body, guard=None, span=None):
        lo, hi = span or (self.lo, self.hi)
        each(lo, hi, lambda t: (guard or self.guard)(t, lambda: body(t)))

    def start(self):
        def part(t):
            for k in self.near:
                self.copy(t, k, self.chip, self.peer(k)).start()
            if self.pair:
                self.pass_on(t, self.chip).start()

        self.parts(part)

    def arrived(self, t, k):
        self.copy(t, k, self.owner(k), self.chip).wait_recv()
        if self.pair:
            self.pass_on(t, self.owner(k)).start()

    def forward(self, span=None):
        def part(t):
            for k in self.near:
                self.arrived(t, k)
                if self.relay:
                    pl.when(self.path(t) == k - 1)(lambda: self.relayed(t, k).start())

        self.parts(part, span=span)

    def forwarded(self, span=None):
        if self.relay:
            self.parts(lambda t: self.arrived(t, 3), span=span)

    def finish(self):
        def sent(t):
            for k in self.near:
                self.copy(t, k, self.chip, self.peer(k)).wait_send()
                if self.relay:
                    pl.when(self.path(t) == k - 1)(lambda: self.relayed(t, k).wait_send())
            if self.pair:
                each(0, self.chips, lambda c: self.pass_on(t, c).wait_send())

        self.parts(sent)
        if self.pair:
            self.parts(
                lambda t: each(
                    0, self.chips, lambda c: self.pass_on(t, c, 1 - self.core).wait_recv()
                ),
                self.other,
            )


def always(t, body):
    body()


class Gather(Item):
    def __init__(self, sizes, array, split_axes, stages, half=False):
        self.sizes, self.split_axes, self.stages, self.half = sizes, split_axes, stages, half
        self.shards = sizes["shard"]
        self.slots = self.shards // 2 if half else self.shards
        self.pair = len(split_axes) == 2
        both = stages == "both"
        self.pre = 0 if stages == "plane" or half else 1
        self.inputs = [array]
        self.in_specs = [VMEM_SPEC if both else HBM_SPEC]
        if stages == "plane":
            shape, self.aliased = tuple(array.shape), True
        else:
            shape = (self.slots,) + tuple(array.shape)
        self.out_shapes = [jax.ShapeDtypeStruct(shape, array.dtype)]
        self.out_specs = [VMEM_SPEC if both else HBM_SPEC]
        dma = pltpu.SemaphoreType.DMA
        self.scratch = []
        if stages != "plane":
            self.scratch += [dma((self.shards,)), dma((self.shards,))]
        if stages == "z":
            self.scratch += [pltpu.VMEM(array.shape, array.dtype), dma((2,))]
        else:
            self.plane = Plane(sizes, self.pair, 1, self.shards)
            self.scratch += self.plane.scratch

    def guarded(self, z, body):
        if self.half:
            pl.when(z // self.slots == lax.axis_index("core"))(body)
        else:
            body()

    def slot(self, z):
        return lax.rem(z, self.slots) if self.half else z

    def z_copy(self, k, src, full, scratch, sending):
        me = lax.axis_index("shard")
        mine = lax.axis_index(self.split_axes)
        peer = lax.rem(me + k, self.shards) if sending else lax.rem(me + self.shards - k, self.shards)
        source = me if sending else peer
        dst = full.at[self.slot(source), mine]
        return remote(
            src.at[mine] if sending else dst,
            dst,
            scratch[0].at[k],
            scratch[1].at[k],
            {"shard": peer},
        )

    def z_start(self, src, full, scratch):
        self.guarded(
            lax.axis_index("shard"),
            lambda: each(1, self.shards, lambda k: self.z_copy(k, src, full, scratch, True).start()),
        )

    def z_finish(self, src, full, scratch):
        me = lax.axis_index("shard")

        def receive(k):
            peer = lax.rem(me + self.shards - k, self.shards)
            self.guarded(
                peer, lambda: self.z_copy(k, src, full, scratch, False).wait_recv()
            )

        each(1, self.shards, receive)

        def sent():
            each(1, self.shards, lambda k: self.z_copy(k, src, full, scratch, True).wait_send())

        self.guarded(me, sent)

    def steps(self, ins, outs, scratch):
        me = lax.axis_index("shard")
        src, full = ins[0], outs[0]
        if self.stages == "z":
            self.z_start(src, full, scratch)
            load = pltpu.make_async_copy(src, scratch[2], scratch[3].at[0])
            store = pltpu.make_async_copy(scratch[2], full.at[self.slot(me)], scratch[3].at[1])
            self.guarded(me, load.start)
            yield

            def both():
                load.wait()
                store.start()

            self.guarded(me, both)
            yield
            self.guarded(me, store.wait)
            self.z_finish(src, full, scratch)
            return

        def shard_of(t):
            return lax.rem(me + t, self.shards)

        def region(t, chip, core):
            return full.at[self.slot(shard_of(t)), 2 * chip + core if self.pair else chip]

        guard = (lambda t, body: self.guarded(shard_of(t), body)) if self.half else always
        if self.stages == "both":
            self.z_start(src, full, scratch)

            def keep():
                full[self.slot(me)] = src[...]

            self.guarded(me, keep)
        self.plane.bind(
            region, lambda t: lax.rem(shard_of(t), 2), guard, always, scratch[-len(self.plane.scratch) :]
        )
        if self.stages == "both":
            yield
            self.z_finish(src, full, scratch)
        self.plane.start()
        yield
        self.plane.forward()
        yield
        self.plane.forwarded()
        yield
        self.plane.finish()


class ChunkGather(Item):
    aliased = True
    final = True

    def __init__(self, sizes, array):
        self.shards, self.chunks = sizes["shard"], array.shape[2]
        self.each = self.shards - 1
        self.inputs, self.in_specs = [array], [HBM_SPEC]
        self.out_shapes = [jax.ShapeDtypeStruct(array.shape, array.dtype)]
        self.out_specs = [HBM_SPEC]
        self.plane = Plane(sizes, False, 0, self.chunks * self.each)
        self.scratch = self.plane.scratch

    def span(self, c):
        return (c * self.each, (c + 1) * self.each)

    def forward(self, c):
        self.plane.forward(self.span(c))

    def arrived(self, c):
        self.plane.forwarded(self.span(c))

    def steps(self, ins, outs, scratch):
        me = lax.axis_index("shard")

        def shard_of(t):
            return lax.rem(me + 1 + lax.rem(t, self.each), self.shards)

        self.plane.bind(
            lambda t, chip, core: outs[0].at[shard_of(t), chip, t // self.each],
            lambda t: lax.rem(shard_of(t), 2),
            always,
            always,
            scratch,
        )
        self.plane.start()
        yield
        self.plane.finish()


class Reduce(Item):
    def __init__(self, sizes, array, stages, half=False, late=False, source=None):
        self.stages, self.half, self.late, self.source = stages, half, late, source
        self.pre = int(stages[0] == "pair" and not late)
        self.chips, self.shards = sizes["chip"], sizes["shard"]
        self.slots = self.shards // 2
        lead = {"pair": 3, "plane": 2, "shard": 1, "spread": 0}[stages[0]]
        unit = tuple(array.shape[lead:])
        self.zs = array.shape[0]
        zs, chips, dtype = self.zs, self.chips, array.dtype
        self.inputs = [] if source is not None else [array]
        self.from_hbm = source is None and stages[0] == "plane"
        self.relay = chips == 4 and not late and "plane" in stages
        self.in_specs = [HBM_SPEC if self.from_hbm else VMEM_SPEC] * len(self.inputs)
        self.names, self.scratch = [], []

        def add(name, buffer):
            self.names.append(name)
            self.scratch.append(buffer)

        dma = pltpu.SemaphoreType.DMA
        if "pair" in stages:
            add("pair_got", pltpu.VMEM((zs, chips) + unit, dtype))
            add("pair_sum", pltpu.VMEM((zs, chips) + unit, dtype))
            add("pair_sems", dma((2,)))
        if self.relay:
            half_unit = (zs,) + unit[1:]
            add("near_got", pltpu.VMEM((2, 2) + half_unit, dtype))
            add("relay_sum", pltpu.VMEM((2,) + half_unit, dtype))
            add("relay_got", pltpu.VMEM((2,) + half_unit, dtype))
            add("near_sent", dma((2, 2)))
            add("near_arrived", dma((2, 2)))
            add("relay_sent", dma((2,)))
            add("relay_arrived", dma((2,)))
            if self.from_hbm:
                add("plane_own", pltpu.VMEM((zs,) + unit, dtype))
                add("far_own", pltpu.VMEM((2,) + half_unit, dtype))
                add("own_sems", dma((3,)))
            if stages[-1] != "plane":
                add("plane_sum", pltpu.VMEM((zs,) + unit, dtype))
        elif "plane" in stages:
            add("plane_got", pltpu.VMEM((chips - 1, zs) + unit, dtype))
            add("plane_sent", dma((chips,)))
            add("plane_arrived", dma((chips,)))
            if self.from_hbm:
                add("plane_own", pltpu.VMEM((zs,) + unit, dtype))
                add("own_sems", dma((1,)))
            if stages[-1] != "plane":
                add("plane_sum", pltpu.VMEM((zs,) + unit, dtype))
        if "shard" in stages:
            add("shard_got", pltpu.VMEM((self.shards - 1,) + unit, dtype))
            add("shard_sent", dma((self.shards,)))
            add("shard_arrived", dma((self.shards,)))
        shape = (zs,) + unit if stages[-1] == "plane" else unit
        if stages[-1] == "spread":
            shape = (chips,) + (() if half else (2,)) + unit
            self.plane = Plane(sizes, True, 0, unit[0])
            for index, buffer in enumerate(self.plane.scratch):
                add("spread%d" % index, buffer)
        self.out_shapes = [jax.ShapeDtypeStruct(shape, dtype)]
        self.out_specs = [VMEM_SPEC]

    def steps(self, ins, outs, scratch):
        buf = types.SimpleNamespace(**dict(zip(self.names, scratch)))
        chip, core, shard = (lax.axis_index(name) for name in ALL)
        now, out, last, sent = ins[0], outs[0], self.stages[-1], []
        mine = out.at[chip] if self.half else out.at[chip, core]

        def carrying(index):
            return index // self.slots == core

        def guard(t, body):
            if self.half:
                pl.when(carrying(shard))(body)
            else:
                body()

        def other(t, body):
            if self.half:
                pl.when(jnp.logical_not(carrying(shard)))(body)
            else:
                body()

        if "pair" in self.stages:
            pair = remote(
                now.at[:, :, 1 - core],
                buf.pair_got,
                buf.pair_sems.at[0],
                buf.pair_sems.at[1],
                {"core": 1 - core},
            )
            pair.start()
            yield
            pair.wait()
            given = now

            def add_pair(index):
                z, c = index // self.chips, lax.rem(index, self.chips)
                total = given[z, c, core].astype(f32) + buf.pair_got[z, c].astype(f32)
                buf.pair_sum[z, c] = total.astype(bf16)

            each(0, self.zs * self.chips, add_pair)
            now = buf.pair_sum
        if self.relay:
            source, target = now, out if last == "plane" else buf.plane_sum

            def near_copy(part, dest):
                near = flipped(chip, part + 1)
                return remote(
                    source.at[:, near if dest == 0 else flipped(chip, 3), part],
                    buf.near_got.at[part, dest],
                    buf.near_sent.at[part, dest],
                    buf.near_arrived.at[part, dest],
                    {"chip": near},
                )

            def relay_copy(part):
                return remote(
                    buf.relay_sum.at[part],
                    buf.relay_got.at[part],
                    buf.relay_sent.at[part],
                    buf.relay_arrived.at[part],
                    {"chip": flipped(chip, 2 - part)},
                )

            def own_copies():
                copies = [(source.at[:, chip], buf.plane_own)]
                for part in range(2):
                    far = flipped(chip, 2 - part)
                    copies.append((source.at[:, far, part], buf.far_own.at[part]))
                return [
                    pltpu.make_async_copy(src, dst, buf.own_sems.at[index])
                    for index, (src, dst) in enumerate(copies)
                ]

            for dest in (1, 0):
                for part in range(2):
                    near_copy(part, dest).start()
            if self.from_hbm:
                for copy in own_copies():
                    copy.start()
            yield
            if self.from_hbm:
                for copy in own_copies():
                    copy.wait()
            for part in range(2):
                near_copy(part, 1).wait_recv()
                far = flipped(chip, 2 - part)

                def add_far(z):
                    own = buf.far_own[part, z] if self.from_hbm else source[z, far, part]
                    total = own.astype(f32) + buf.near_got[part, 1, z].astype(f32)
                    buf.relay_sum[part, z] = total.astype(bf16)

                each(0, self.zs, add_far)
                relay_copy(part).start()
            yield
            for part in range(2):
                near_copy(part, 0).wait_recv()
                relay_copy(part).wait_recv()

                def add_near(z):
                    own = buf.plane_own[z, part] if self.from_hbm else source[z, chip, part]
                    total = own.astype(f32) + buf.near_got[part, 0, z].astype(f32)
                    target[z, part] = (total + buf.relay_got[part, z].astype(f32)).astype(bf16)

                each(0, self.zs, add_near)

            def relay_sent():
                for part in range(2):
                    relay_copy(part).wait_send()
                    for dest in range(2):
                        near_copy(part, dest).wait_send()

            sent.append(relay_sent)
            now = target
        elif "plane" in self.stages:
            partial = now

            def plane_copy(k):
                peer = lax.rem(chip + k, self.chips)
                return remote(
                    partial.at[:, peer],
                    buf.plane_got.at[k - 1],
                    buf.plane_sent.at[k],
                    buf.plane_arrived.at[k],
                    {"chip": peer},
                )

            each(1, self.chips, lambda k: plane_copy(k).start())
            if self.from_hbm:
                own = pltpu.make_async_copy(
                    partial.at[:, chip], buf.plane_own, buf.own_sems.at[0]
                )
                own.start()
            yield
            each(1, self.chips, lambda k: plane_copy(k).wait_recv())
            if self.from_hbm:
                own.wait()
            target = out if last == "plane" else buf.plane_sum

            def add_plane(z):
                total = (buf.plane_own[z] if self.from_hbm else partial[z, chip]).astype(f32)
                for k in range(self.chips - 1):
                    total = total + buf.plane_got[k, z].astype(f32)
                target[z] = total.astype(bf16)

            each(0, self.zs, add_plane)
            sent.append(lambda: each(1, self.chips, lambda k: plane_copy(k).wait_send()))
            now = target
        if "shard" in self.stages:
            summed = now

            def slot(index):
                return lax.rem(index, self.slots) if self.half else index

            def shard_copy(k):
                peer = lax.rem(shard + k, self.shards)
                return peer, remote(
                    summed.at[slot(peer)],
                    buf.shard_got.at[k - 1],
                    buf.shard_sent.at[k],
                    buf.shard_arrived.at[k],
                    {"shard": peer},
                )

            def shard_each(act):
                def one(k):
                    peer, copy = shard_copy(k)
                    if self.half:
                        pl.when(carrying(peer))(lambda: act(copy))
                    else:
                        act(copy)

                each(1, self.shards, one)

            shard_each(lambda copy: copy.start())
            yield

            def add_shard():
                each(1, self.shards, lambda k: shard_copy(k)[1].wait_recv())
                target = mine if last == "spread" else out
                for part in range(target.shape[0]):
                    total = summed[slot(shard), part].astype(f32)
                    for k in range(self.shards - 1):
                        total = total + buf.shard_got[k, part].astype(f32)
                    target[part] = total.astype(bf16)

            guard(0, add_shard)
            sent.append(lambda: shard_each(lambda copy: copy.wait_send()))
        if last == "spread":
            if "shard" not in self.stages:
                mine[...] = now[...]
            self.plane.bind(
                lambda t, c, k: out.at[c, t] if self.half else out.at[c, k, t],
                lambda t: lax.rem(t, 2),
                guard,
                other,
                scratch[-4:],
            )
            self.plane.start()
            yield
            self.plane.forward()
            yield
            self.plane.forwarded()
            yield
            self.plane.finish()
        for wait in sent:
            wait()


class Compute:
    def __init__(self, body, inputs, out_shapes, scratch=()):
        self.body, self.inputs, self.out_shapes = body, list(inputs), list(out_shapes)
        self.scratch = list(scratch)


def greet_all(sizes, wide):
    barrier = pltpu.get_barrier_semaphore()
    groups = [ALL] if wide else [REP, ("shard",)]
    total = 0
    for axes in groups:
        count, me = axes_size(sizes, axes), lax.axis_index(axes)
        total += count - 1

        def greet(k):
            peer = peer_coords(lax.rem(me + k, count), axes, sizes)
            pl.semaphore_signal(barrier, inc=1, device_id=peer, device_id_type=MESH)

        each(1, count, greet)
    pl.semaphore_wait(barrier, total)


DONE = object()


def run(collective_id, name, sizes, items, compute=None, vmem=None):
    wide = any(getattr(item, "axes", ()) == ALL for item in items)
    compute = compute or Compute(None, [], [])
    inputs, in_specs, out_shapes, out_specs, scratch, aliases = [], [], [], [], [], {}
    spans = []
    for item in items:
        if item.aliased:
            aliases[len(inputs)] = len(out_shapes)
        spans.append((len(inputs), len(out_shapes), len(scratch)))
        inputs += item.inputs
        in_specs += item.in_specs
        out_shapes += item.out_shapes
        out_specs += item.out_specs
        scratch += item.scratch
    own = (len(inputs), len(out_shapes), len(scratch))
    inputs += compute.inputs
    in_specs += [VMEM_SPEC] * len(compute.inputs)
    out_shapes += compute.out_shapes
    out_specs += [VMEM_SPEC] * len(compute.out_shapes)
    scratch += compute.scratch
    n_in, n_out = len(inputs), len(out_shapes)

    def kernel(*refs):
        ins, outs, tmp = refs[:n_in], refs[n_in : n_in + n_out], refs[n_in + n_out :]

        def parts(index):
            item, (a, b, c) = items[index], spans[index]
            item_ins = ins[a : a + len(item.inputs)]
            if getattr(item, "source", None) is not None:
                item_ins = [outs[own[1] + item.source]]
            return (
                item_ins,
                outs[b : b + len(item.out_shapes)],
                tmp[c : c + len(item.scratch)],
            )

        greet_all(sizes, wide)
        going = {}
        for index, item in enumerate(items):
            if not item.late:
                going[index] = item.steps(*parts(index))
                next(going[index])
        for index, item in enumerate(items):
            if not item.late:
                for _ in range(item.pre):
                    next(going[index])
        def hook(n):
            for index, item in enumerate(items):
                if n in item.hooks:
                    if index not in going:
                        going[index] = item.steps(*parts(index))
                    next(going[index], DONE)

        hook.outs = [parts(index)[1] for index in range(len(items))]
        if compute.body is not None:
            compute.body(ins[own[0] :], outs[own[1] :], tmp[own[2] :], hook)
        for index, item in enumerate(items):
            if index not in going:
                going[index] = item.steps(*parts(index))
                next(going[index])
        for final in (False, True):
            left = [index for index, item in enumerate(items) if item.final == final]
            while left:
                left = [index for index in left if next(going[index], DONE) is not DONE]

    return pl.pallas_call(
        kernel,
        out_shape=out_shapes,
        in_specs=in_specs,
        out_specs=out_specs,
        scratch_shapes=scratch,
        input_output_aliases=aliases,
        compiler_params=pltpu.CompilerParams(
            collective_id=collective_id, has_side_effects=True, vmem_limit_bytes=vmem
        ),
        name=name,
    )(*inputs)


def mask_rows(code_row):
    index = lax.broadcasted_iota(jnp.int32, (16, code_row.shape[1]), 0)
    return jnp.where(index == code_row, 0.0, NEGATIVE_HUGE).astype(bf16)


def segment_rows(segment_row):
    index = lax.broadcasted_iota(jnp.int32, (16, segment_row.shape[1]), 0)
    return jnp.where(index == segment_row, 1.0, 0.0).astype(bf16)


def as_column(row):
    return jnp.transpose(jnp.broadcast_to(row, (128, row.shape[1])))[:, :1]


def diagonal_bias(info):
    code, place = as_column(info[0:1]), as_column(info[2:3])
    allowed = (place == info[2:3]) | ((code == info[1:2]) & (place <= info[2:3]))
    return jnp.where(allowed, 0.0, NEGATIVE_HUGE)


def forward_body(home, ins, outs, tmp, hook):
    qkv_ref, info_ref = ins
    out_ref, keep_ref, lse_ref = outs
    bias, acc, stat = tmp
    blocks, slots = qkv_ref.shape[0], qkv_ref.shape[1] // 3
    source = key_slots(slots)
    key = [key_unit(slots, source[m]) for m in range(slots)]
    value = [value_unit(slots, source[m]) for m in range(slots)]

    @pl.loop(0, blocks)
    def _(turn):
        i = lax.rem(lax.axis_index(REP) + turn, blocks)
        for n, step in enumerate((blocks // 2, blocks - 2, blocks - 1)):
            pl.when(turn == step)(lambda: hook(n))
        bias[...] = diagonal_bias(info_ref[i])
        seg = segment_rows(info_ref[i, 1:2])
        qa = [jnp.concatenate([qkv_ref[i, m], seg], axis=0) for m in range(slots)]
        for m in range(slots):
            s = dot(jnp.transpose(qkv_ref[i, key[m]]), qkv_ref[i, m]) + bias[...]
            top = jnp.max(s, axis=0, keepdims=True)
            p = jnp.exp(s - top)
            stat[2 * m : 2 * m + 1] = top
            stat[2 * m + 1 : 2 * m + 2] = jnp.sum(p, axis=0, keepdims=True)
            acc[m] = dot(qkv_ref[i, value[m]], p.astype(bf16))

        @pl.loop(0, i)
        def _(j):
            mask = mask_rows(info_ref[j, 0:1])
            for m in range(slots):
                ka = jnp.transpose(jnp.concatenate([qkv_ref[j, key[m]], mask], axis=0))
                s = dot(ka, qa[m])
                old = stat[2 * m : 2 * m + 1]
                top = jnp.maximum(old, jnp.max(s, axis=0, keepdims=True))
                p = jnp.exp(s - top)
                factor = jnp.exp(old - top)
                stat[2 * m : 2 * m + 1] = top
                stat[2 * m + 1 : 2 * m + 2] = stat[2 * m + 1 : 2 * m + 2] * factor + jnp.sum(
                    p, axis=0, keepdims=True
                )
                acc[m] = acc[m] * factor + dot(qkv_ref[j, value[m]], p.astype(bf16))

        for m in range(slots):
            total = stat[2 * m + 1 : 2 * m + 2]
            result = acc[m] / total
            out_ref[i, m] = result.astype(bf16)
            keep_ref[i, m] = result
            lse_ref[i, m : m + 1] = stat[2 * m : 2 * m + 1] + jnp.log(total)
        home.send(i)


def backward_body(ins, outs, tmp, hook):
    qkv_ref, do_ref, keep_ref, lse_ref, info_ref = ins
    (out_ref,) = outs
    bias, dq, qn, don, delta = tmp
    blocks, slots = qkv_ref.shape[0], qkv_ref.shape[1] // 3
    source = key_slots(slots)
    key = [key_unit(slots, source[m]) for m in range(slots)]
    value = [value_unit(slots, source[m]) for m in range(slots)]

    @pl.loop(0, blocks)
    def _(i):
        for m in range(slots):
            qn[i, m] = jnp.transpose(qkv_ref[i, m])
            don[i, m] = jnp.transpose(do_ref[i, m])
            delta[i, m : m + 1] = jnp.sum(
                do_ref[i, m].astype(f32) * keep_ref[i, m], axis=0, keepdims=True
            )
            dq[i, m] = jnp.zeros_like(dq[i, m])

    @pl.loop(0, blocks)
    def _(j):
        for n, step in enumerate((blocks // 2 - 1, blocks // 2, blocks - 2)):
            pl.when(j == step)(lambda: hook(n))
        bias[...] = diagonal_bias(info_ref[j])
        mask = mask_rows(info_ref[j, 0:1])
        kn = [jnp.transpose(qkv_ref[j, key[m]]) for m in range(slots)]
        ka = [
            jnp.transpose(jnp.concatenate([qkv_ref[j, key[m]], mask], axis=0)) for m in range(slots)
        ]
        vn = [jnp.transpose(qkv_ref[j, value[m]]) for m in range(slots)]

        def tile(i, m, s):
            p = jnp.exp(s - lse_ref[i, m : m + 1])
            dp = dot(vn[m], do_ref[i, m])
            ds = (p * (dp - delta[i, m : m + 1])).astype(bf16)
            dq[i, m] += dot(qkv_ref[j, key[m]], ds)
            return dot(ds, qn[i, m]), dot(p.astype(bf16), don[i, m])

        start = []
        for m in range(slots):
            start += list(tile(j, m, dot(kn[m], qkv_ref[j, m]) + bias[...]))

        def later(i, carry):
            seg = segment_rows(info_ref[i, 1:2])
            new = []
            for m in range(slots):
                qa = jnp.concatenate([qkv_ref[i, m], seg], axis=0)
                a, b = tile(i, m, dot(ka[m], qa))
                new += [carry[2 * m] + a, carry[2 * m + 1] + b]
            return tuple(new)

        done = lax.fori_loop(j + 1, blocks, later, tuple(start))
        done = [jnp.transpose(value) for value in done]
        if slots == 2:
            shared = (1 - source[1]).astype(f32)
            done[0] = done[0] + done[2] * shared
            done[1] = done[1] + done[3] * shared
        for m in range(slots):
            out_ref[j, key_unit(slots, m)] = done[2 * m].astype(bf16)
            out_ref[j, value_unit(slots, m)] = done[2 * m + 1].astype(bf16)

    @pl.loop(0, blocks)
    def _(i):
        for m in range(slots):
            out_ref[i, m] = (dq[i, m] * HEAD_DIM ** (-0.5)).astype(bf16)


def ffn_body(late, ins, outs, tmp, hook):
    first_ref, down_ref, attn_ref, out_ref, hidden_ref, grad_ref, scale_ref, gain_ref = ins
    gu_grad_ref, down_grad_ref, part_ref, branch_ref = outs
    raw, weight, ffn, dx, sem = tmp
    (x_ref,), (gf_ref,), (late_ref,) = hook.outs[:3]
    cores, rows, width = x_ref.shape
    core = lax.axis_index("core")
    shards, filled = raw.shape[0], width // raw.shape[0]
    columns = weight.shape[1]
    half = columns // 2
    padded = raw.shape[1] * raw.shape[2]

    @pl.loop(0, rows // 128)
    def _(block):
        at = pl.ds(pl.multiple_of(block * 128, 128), 128)
        branch = dot(attn_ref[:filled, at], out_ref[0, :filled], 0, 0)
        for z in range(1, shards):
            here = attn_ref[z * filled : (z + 1) * filled, at]
            branch = branch + dot(here, out_ref[z, :filled], 0, 0)
        branch_ref[at] = branch
        x_ref[core, at] = rms_scale(hidden_ref[at].astype(f32) + branch, gain_ref[...]).astype(bf16)
        gf_ref[core, at] = (scale_ref[at] * grad_ref[at].astype(f32)).astype(bf16)

    hook(0)

    def compact(get):
        for z in range(shards):
            weight[z * filled : (z + 1) * filled] = get(z)[:filled]

    compact(lambda z: first_ref[z].reshape(padded, columns))
    hook(1)
    x = x_ref[...].reshape(cores * rows, width)
    gf = gf_ref[...].reshape(cores * rows, width)

    @pl.loop(0, late.chunks + 1)
    def _(k):
        at = pl.multiple_of(k * columns, columns)
        down = down_ref[pl.ds(pl.multiple_of(k * half, half), half)]

        @pl.when(k < late.chunks)
        def _():
            late.forward(k)

        both = dot(x, weight[...])
        gate, up = both[:, :half], both[:, half:]
        sig = 1.0 / (1.0 + jnp.exp(-gate))
        act = gate * sig
        hidden = (act * up).astype(bf16)
        grad_hidden = dot(gf, down, 1, 1)
        grad_gate = (grad_hidden * up * (sig * (1.0 + gate * (1.0 - sig)))).astype(bf16)
        grad_up = (grad_hidden * act).astype(bf16)
        grads = jnp.concatenate([grad_gate, grad_up], axis=1)
        ffn_now = dot(hidden, down)
        dx_now = dot(grads, weight[...], 1, 1)

        @pl.when(k == 0)
        def _():
            ffn[...] = ffn_now
            dx[...] = dx_now

        @pl.when(k > 0)
        def _():
            ffn[...] += ffn_now
            dx[...] += dx_now

        @pl.when(k == late.chunks)
        def _():
            for c in range(cores):
                part_ref[c, 0] = dx[c * rows : (c + 1) * rows].astype(bf16)
                part_ref[c, 1] = ffn[c * rows : (c + 1) * rows].astype(bf16)
            hook(2)

        load = pltpu.make_async_copy(late_ref.at[:, :, jnp.minimum(k, late.chunks - 1)], raw, sem.at[0])

        @pl.when(k < late.chunks)
        def _():
            late.arrived(k)
            load.start()

        gu_grad = dot(x, grads, 0, 0)
        for z in range(shards):
            gu_grad_ref[z, :filled, pl.ds(at, columns)] = gu_grad[
                z * filled : (z + 1) * filled
            ].astype(bf16)
            if padded > filled:
                gu_grad_ref[z, filled:, pl.ds(at, columns)] = jnp.zeros(
                    (padded - filled, columns), bf16
                )
        down_grad_ref[pl.ds(pl.multiple_of(k * half, half), half)] = dot(hidden, gf, 0, 0).astype(
            bf16
        )

        @pl.when(k < late.chunks)
        def _():
            load.wait()
            compact(lambda z: raw[z].reshape(padded, columns))


def rms_scale(rows, gain):
    return rows * lax.rsqrt(jnp.mean(rows * rows, axis=-1, keepdims=True) + EPSILON) * gain


def norm_back(rows, gain, grad):
    r = lax.rsqrt(jnp.mean(rows * rows, axis=-1, keepdims=True) + EPSILON)
    scaled = gain * grad
    back = r * scaled - rows * (r * r * r) * jnp.mean(scaled * rows, axis=-1, keepdims=True)
    return back, jnp.sum(grad * rows * r, axis=0)


def line_layout(lengths_row, positions):
    seq_ends = jnp.cumsum(lengths_row, dtype=jnp.int32)
    reached = seq_ends[None, :] <= positions[:, None]
    segment = jnp.sum(reached.astype(jnp.int32), axis=1)
    starts = jnp.max(jnp.where(reached, seq_ends[None, :], 0), axis=1)
    return segment, positions - starts, positions < seq_ends[-1]


def project_body(ins, outs, tmp, hook):
    hidden_ref, weight_ref, gain_ref, cos_ref, sin_ref = ins
    sent_ref, normed_ref, full_ref = outs
    reps, units, _, rows = sent_ref.shape
    slots, filled = units // 3, full_ref.shape[0] // weight_ref.shape[0]
    for z in range(weight_ref.shape[0]):
        full_ref[z * filled : (z + 1) * filled] = weight_ref[z, :filled]
    hidden = hidden_ref[...].astype(f32)
    normed = rms_scale(hidden, gain_ref[...]).astype(bf16)
    normed_ref[...] = normed
    cosines, sines = cos_ref[...], sin_ref[...]
    half, columns = HEAD_DIM // 2, full_ref.shape[1]

    def put(kind, head, value):
        slot = head % slots
        unit = (slot, key_unit(slots, slot), value_unit(slots, slot))[kind]
        sent_ref[head // slots, unit] = value

    for start in range(0, columns, 256):
        stop = min(start + 256, columns)
        block = jnp.transpose(dot(normed, full_ref[:, start:stop]))
        for head in range(start // HEAD_DIM, stop // HEAD_DIM):
            at = head * HEAD_DIM - start
            a, b = block[at : at + half], block[at + half : at + HEAD_DIM]
            if head < QUERY_HEADS:
                scale = HEAD_DIM ** (-0.5)
                put(
                    0,
                    head,
                    (
                        jnp.concatenate(
                            [a * cosines - b * sines, b * cosines + a * sines], axis=0
                        )
                        * scale
                    ).astype(bf16),
                )
            elif head < QUERY_HEADS + KEY_VALUE_HEADS:
                value = jnp.concatenate(
                    [a * cosines - b * sines, b * cosines + a * sines], axis=0
                ).astype(bf16)
                for m in range(GROUP):
                    put(1, (head - QUERY_HEADS) * GROUP + m, value)
            else:
                value = block[at : at + HEAD_DIM].astype(bf16)
                for m in range(GROUP):
                    put(2, (head - QUERY_HEADS - KEY_VALUE_HEADS) * GROUP + m, value)
    for head in range(QUERY_HEADS, reps * slots):
        for kind in range(3):
            put(kind, head, jnp.zeros((HEAD_DIM, rows), bf16))


def project_back_body(ins, outs, tmp, hook):
    (grads_ref, cos_ref, sin_ref, weight_ref, hidden_ref, normed_ref, gain_ref, base_ref) = ins[:8]
    vectors_ref = ins[8]
    sent_ref, weight_grad_ref, vectors_grad_ref = outs
    (dt,) = tmp
    slots, half = grads_ref.shape[1] // 3, HEAD_DIM // 2
    cosines, sines = cos_ref[...], sin_ref[...]

    def get(kind, head):
        slot = head % slots
        unit = (slot, key_unit(slots, slot), value_unit(slots, slot))[kind]
        return grads_ref[head // slots, unit].astype(f32)

    def back(value):
        a, b = value[:half], value[half:]
        return jnp.concatenate([a * cosines + b * sines, b * cosines - a * sines], axis=0)

    for head in range(QUERY_HEADS):
        dt[head * HEAD_DIM : (head + 1) * HEAD_DIM] = back(get(0, head)).astype(bf16)
    for group in range(KEY_VALUE_HEADS):
        for kind in (1, 2):
            value = get(kind, group * GROUP)
            for head in range(group * GROUP + 1, (group + 1) * GROUP):
                if slots != 2 or head % 2 == 0:
                    value = value + get(kind, head)
            if kind == 1:
                value = back(value)
            at = (QUERY_HEADS + (kind - 1) * KEY_VALUE_HEADS + group) * HEAD_DIM
            dt[at : at + HEAD_DIM] = value.astype(bf16)
    grad = dot(dt[...], weight_ref[...], 0, 1)
    norm_grad, gain_grad = norm_back(hidden_ref[...].astype(f32), gain_ref[...], grad)
    index = lax.broadcasted_iota(jnp.int32, vectors_ref.shape, 0)
    vectors = jnp.where(index == 0, gain_grad[None], vectors_ref[...])
    piece = vectors_grad_ref.shape[2]
    for z in range(vectors_grad_ref.shape[0]):
        vectors_grad_ref[z] = vectors[:, z * piece : (z + 1) * piece]
    total = (base_ref[...] + norm_grad).astype(bf16)
    devices, per_pair = sent_ref.shape[:2]
    sent_ref[...] = total.reshape(sent_ref.shape)
    hook(0)
    shards, chips, cores, parts, unit, columns = weight_grad_ref.shape
    filled = normed_ref.shape[1] // shards
    places = [(c, k, p) for c in range(chips) for k in range(cores) for p in range(parts)]
    for start in range(0, columns, 256):
        stop = min(start + 256, columns)
        block = dot(normed_ref[...], dt[start:stop], 0, 1)
        for z in range(shards):
            for r, place in enumerate(places):
                size = max(0, min(unit, filled - r * unit))
                at = z * filled + r * unit
                here = weight_grad_ref.at[z, *place]
                if size:
                    here[:size, start:stop] = block[at : at + size].astype(bf16)
                if size < unit:
                    here[size:, start:stop] = jnp.zeros((unit - size, stop - start), bf16)


def prepare_body(ins, outs, tmp, hook):
    to_slot_ref, cotangent_ref, gate_ref, up_ref, down_ref = ins
    slots_ref, first_ref, late_ref, down_rows_ref = outs
    hook(0)
    sent = dot(to_slot_ref[...], cotangent_ref[...]).astype(bf16)
    slots_ref[...] = sent.reshape(slots_ref.shape)
    chips, unit = first_ref.shape[:2]
    filled, half = gate_ref.shape[0], gate_ref.shape[1] // 2
    for chip in range(chips):
        size = max(0, min(unit, filled - chip * unit))
        for chunk in range(late_ref.shape[1] + 1):
            target = late_ref.at[chip, chunk - 1] if chunk else first_ref.at[chip]
            at = pl.multiple_of(lax.axis_index("core") * half + chunk * FF_CHUNK, FF_CHUNK)
            for which, source in enumerate((gate_ref, up_ref)):
                columns = pl.ds(which * FF_CHUNK, FF_CHUNK)
                if size:
                    rows = pl.ds(chip * unit, size)
                    target[:size, columns] = source[rows, pl.ds(at, FF_CHUNK)]
                if size < unit:
                    target[size:, columns] = jnp.zeros((unit - size, FF_CHUNK), bf16)
    count = down_rows_ref.shape[0]
    for start in range(0, count, 128):
        stop = min(start + 128, count)
        down_rows_ref[start:stop] = jnp.transpose(down_ref[:, start:stop])


def grads_body(ins, outs, tmp, hook):
    (parts_ref, hidden_ref, branch_ref, grad_ref, scale_ref, logit_ref, gain_ref, router_ref) = ins[:8]
    out_weight_ref, attn_ref = ins[8:]
    sent_ref, result_ref, base_ref, vectors_ref, out_grad_ref = outs
    (grad_attn,) = tmp
    rows, width = hidden_ref.shape
    group = 64 // result_ref.shape[1]

    def block(b, carry):
        at = pl.ds(pl.multiple_of(b * 64, 64), 64)
        hidden, branch = hidden_ref[at].astype(f32), branch_ref[at]
        grad, scale = grad_ref[at].astype(f32), scale_ref[at]
        grad_normed = parts_ref[0, 0, at].astype(f32) + parts_ref[1, 0, at].astype(f32)
        ffn = parts_ref[0, 1, at].astype(f32) + parts_ref[1, 1, at].astype(f32)
        total = branch + ffn
        result = (hidden + scale * total).astype(bf16)
        result_ref[pl.ds(b * group, group)] = result.reshape(group, *result_ref.shape[1:])
        grad_logit = logit_ref[at] * jnp.sum(grad * total, axis=1, keepdims=True)
        grad_middle, gain_grad = norm_back(hidden + branch, gain_ref[...], grad_normed)
        grad_attn[at] = (scale * grad + grad_middle).astype(bf16)
        base_ref[at] = grad + grad_middle + grad_logit * router_ref[...]
        router_grad = jnp.sum(grad_logit * hidden, axis=0)
        return carry[0] + gain_grad[None], carry[1] + router_grad[None]

    zero = jnp.zeros((1, width), f32)
    gain_grad, router_grad = lax.fori_loop(0, rows // 64, block, (zero, zero))
    index = lax.broadcasted_iota(jnp.int32, vectors_ref.shape, 0)
    vectors_ref[...] = jnp.where(index == 1, gain_grad, jnp.where(index == 2, router_grad, 0.0))
    reps, slots = sent_ref.shape[:2]
    shards, filled = out_weight_ref.shape[0], width // out_weight_ref.shape[0]
    for z in range(shards):
        piece = dot(out_weight_ref[z, :filled], grad_attn[...], 1, 1).astype(bf16)
        start = z * filled
        while start < (z + 1) * filled:
            head = start // HEAD_DIM
            stop = min((head + 1) * HEAD_DIM, (z + 1) * filled)
            rows_of_head = pl.ds(start - head * HEAD_DIM, stop - start)
            sent_ref[head // slots, head % slots, rows_of_head] = piece[
                start - z * filled : stop - z * filled
            ]
            start = stop
    for head in range(width // HEAD_DIM, reps * slots):
        sent_ref[head // slots, head % slots] = jnp.zeros(sent_ref.shape[2:], bf16)
    hook(0)
    _, chips, cores, parts, unit, _ = out_grad_ref.shape
    places = [(c, k, p) for c in range(chips) for k in range(cores) for p in range(parts)]
    for z in range(shards):
        piece = dot(attn_ref[z * filled : (z + 1) * filled], grad_attn[...])
        for r, place in enumerate(places):
            size = max(0, min(unit, filled - r * unit))
            here = out_grad_ref.at[z, *place]
            if size:
                here[:size] = piece[r * unit : r * unit + size].astype(bf16)
            if size < unit:
                here[size:] = jnp.zeros((unit - size, width), bf16)


def finalize_kernel(*refs):
    gate_up_ref, down_ref, out_ref, qkv_ref, slot_ref, result_ref, grad_ref = refs[:7]
    gate, up, down, out, query, key, value, result, grad = refs[7:]
    lanes = lax.broadcasted_iota(jnp.int32, (slot_ref.shape[0], result_ref.shape[0]), 1)
    from_slot = jnp.where(lanes == slot_ref[...], 1.0, 0.0).astype(bf16)
    result[...] = dot(from_slot, result_ref[...]).astype(bf16)
    grad[...] = dot(from_slot, grad_ref[...]).astype(bf16)
    cores, rows, columns = gate_up_ref.shape[1:]
    half = columns // 2
    for core in range(cores):
        for start in range(0, columns, 2 * FF_CHUNK):
            at = core * half + start // 2
            middle = start + FF_CHUNK
            gate[:, at : at + FF_CHUNK] = gate_up_ref[0, core, :, start:middle].astype(f32)
            up[:, at : at + FF_CHUNK] = gate_up_ref[0, core, :, middle : middle + FF_CHUNK].astype(f32)
    down[...] = down_ref[0].astype(f32)
    out[...] = out_ref[0].astype(f32)
    ends = (query.shape[1], query.shape[1] + key.shape[1])
    qkv = qkv_ref[0].astype(f32)
    query[...] = qkv[:, : ends[0]]
    key[...] = qkv[:, ends[0] : ends[1]]
    value[...] = qkv[:, ends[1] :]


def finalize(gate_up, down, out, qkv, slot_of_row, result, grad, shard_rows, key_width):
    chips, rows = gate_up.shape[0], gate_up.shape[2]
    width, hidden = out.shape[2], gate_up.shape[3]
    columns = (hidden, hidden, None, width, width, key_width, key_width)
    count = result.shape[0] // chips

    def out_spec(array_columns):
        shape = tuple(down.shape[1:]) if array_columns is None else (rows, array_columns)
        return pl.BlockSpec(shape, lambda c: (c, 0))

    def out_type(array_columns):
        shape = (chips * down.shape[1], down.shape[2])
        shape = shape if array_columns is None else (shard_rows, array_columns)
        return jax.ShapeDtypeStruct(shape, f32)

    return pl.pallas_call(
        finalize_kernel,
        grid=(chips,),
        in_specs=[pl.BlockSpec((1, 2, rows, hidden), lambda c: (c, 0, 0, 0))]
        + [pl.BlockSpec((1,) + tuple(a.shape[1:]), lambda c: (c, 0, 0)) for a in (down, out, qkv)]
        + [pl.BlockSpec((count, 1), lambda c: (c, 0))]
        + [pl.BlockSpec(result.shape, lambda c: (0, 0))] * 2,
        out_specs=[out_spec(c) for c in columns]
        + [pl.BlockSpec((count, width), lambda c: (c, 0))] * 2,
        out_shape=[out_type(c) for c in columns] + [jax.ShapeDtypeStruct(result.shape, bf16)] * 2,
        name="finalize",
    )(gate_up, down, out, qkv, slot_of_row[:, None], result, grad)


def rounded_up(value, unit):
    return -(-value // unit) * unit


def local(
    sizes,
    hidden_in,
    cotangent,
    destination,
    seq_lengths,
    gate_mask,
    query_weight,
    key_matrix,
    value_matrix,
    out_weight,
    gate_weight,
    up_weight,
    down_weight,
    attn_gain,
    ffn_gain,
    router_weight,
):
    rows, width = hidden_in.shape
    chips, shards = sizes["chip"], sizes["shard"]
    reps = 2 * chips
    devices = reps * shards
    per_pair = rows // devices
    slots = -(-QUERY_HEADS // reps)
    padded_heads = slots * reps
    chip, core, shard = lax.axis_index("chip"), lax.axis_index("core"), lax.axis_index("shard")
    rep = lax.axis_index(REP)
    shard_rows = query_weight.shape[0]
    rep_unit = rounded_up(-(-shard_rows // reps), 8)
    padded = rep_unit * reps
    chip_unit = padded // chips
    ff_half = gate_weight.shape[1] // 2
    chunks = ff_half // FF_CHUNK

    def padded_rows(array):
        return jnp.pad(array, ((0, padded - shard_rows), (0, 0)))

    qkv_shard = padded_rows(jnp.concatenate([query_weight, key_matrix, value_matrix], axis=1))
    qkv_shard = qkv_shard.reshape(reps, rep_unit, -1)
    out_shard = padded_rows(out_weight).reshape(reps, rep_unit, width)
    down_unit = down_weight.shape[0] // chips
    vectors = jnp.stack([attn_gain, ffn_gain, router_weight]).astype(f32)
    vectors = jnp.pad(vectors, ((0, 5), (0, 0)))

    row_index = jnp.arange(rows, dtype=jnp.int32)
    target = destination // rows
    earlier = (target[None, :] == target[:, None]) & (row_index[None, :] < row_index[:, None])
    slot_of_row = target * per_pair + jnp.sum(earlier.astype(jnp.int32), axis=1)
    to_slot = slot_of_row[None, :] == row_index[:, None]
    to_slot_b = to_slot.astype(bf16)
    place_sent = jnp.sum(jnp.where(to_slot, (destination % rows)[None, :], 0), axis=1)
    place_sent = place_sent.reshape(devices, 1, per_pair)
    place_sent = jnp.pad(place_sent, ((0, 0), (0, 0), (0, 128 - per_pair)))

    def by_slot(tokens):
        tokens = jnp.dot(to_slot_b, tokens, preferred_element_type=f32).astype(bf16)
        return tokens.reshape(devices, per_pair, width)

    first_type = jax.ShapeDtypeStruct((chips, chip_unit, 2 * FF_CHUNK), bf16)
    late_type = jax.ShapeDtypeStruct((chips, chunks - 1, chip_unit, 2 * FF_CHUNK), bf16)
    tokens_type = jax.ShapeDtypeStruct((devices, per_pair, width), bf16)
    got_hidden, got_place, vectors_got, qkv_full, grad_slots, first_shard, late_shard, down_shard = run(
        1,
        "first",
        sizes,
        [
            AllToAll(sizes, by_slot(hidden_in), ALL, late=True).at(0),
            AllToAll(sizes, place_sent, ALL, late=True).at(0),
            AllToAll(sizes, vectors, ("shard",), spread=True),
            Gather(sizes, qkv_shard, REP, "both"),
        ],
        Compute(
            prepare_body,
            [to_slot_b, cotangent, gate_weight, up_weight, jnp.transpose(down_weight)],
            [
                tokens_type,
                first_type,
                late_type,
                jax.ShapeDtypeStruct(down_weight.shape, bf16),
            ],
        ),
    )
    down_shard = down_shard.reshape(chips, down_unit, width)
    hidden = got_hidden.reshape(rows, width)
    place = got_place[:, 0, :per_pair].reshape(rows)
    qkv_full = qkv_full.reshape(shards, padded, -1)
    vectors_full = jnp.transpose(vectors_got[:, :3], (1, 0, 2)).reshape(3, width)
    gain_one, gain_two, full_router = vectors_full[0], vectors_full[1], vectors_full[2]
    router_logit = jnp.sum(hidden.astype(f32) * full_router, axis=1)
    gate_value = jax.nn.sigmoid(router_logit)

    positions = rep * rows + place
    segment, within, is_valid = line_layout(seq_lengths[0], positions)
    here = place[:, None] == row_index[None, :]
    gate_here = jnp.sum(jnp.where(here, gate_mask[None, :], 0), axis=1)
    active = is_valid & (gate_here == 1)
    key_code = jnp.where(active, segment, -1)
    active_f = active.astype(f32)
    branch_scale = (active_f * gate_value)[:, None]
    logit_scale = branch_scale * (1.0 - gate_value)[:, None]
    info = jnp.pad(jnp.stack([key_code, segment, place]), ((0, 5), (0, 0)))
    steps = jnp.arange(HEAD_DIM // 2).astype(f32)
    frequency = jnp.power(ROPE_BASE, -2.0 * steps / HEAD_DIM)
    angles = frequency[:, None] * within.astype(f32)[None, :]
    cosines, sines = jnp.cos(angles), jnp.sin(angles)

    heads_shape = (reps, 3 * slots, HEAD_DIM, rows)
    heads_type = jax.ShapeDtypeStruct(heads_shape, bf16)
    first_z, late_z, out_z, info_got, qkv_got, _, first_normalized, qkv_weights = run(
        2,
        "project",
        sizes,
        [
            Gather(sizes, first_shard, ("chip",), "z"),
            Gather(sizes, late_shard, ("chip",), "z"),
            Gather(sizes, out_shard, REP, "z"),
            AllToAll(sizes, info, REP, spread=True),
            Heads(sizes, heads_type, True, 0),
        ],
        Compute(
            project_body,
            [hidden, qkv_full, gain_one[None], cosines, sines],
            [
                heads_type,
                jax.ShapeDtypeStruct((rows, width), bf16),
                jax.ShapeDtypeStruct((width, qkv_full.shape[2]), bf16),
            ],
        ),
    )
    slot_type = jax.ShapeDtypeStruct((reps, slots, HEAD_DIM, rows), bf16)
    home = Stepwise(sizes, slot_type, 0)
    first_full, down_full, out_full, got_grad, att_home, _, att_keep, lse = run(
        3,
        "attend",
        sizes,
        [
            Gather(sizes, first_z, ("chip",), "plane").at(1),
            Gather(sizes, down_shard, ("chip",), "both", half=True).at(0, 2),
            Gather(sizes, out_z, REP, "plane").at(1),
            AllToAll(sizes, grad_slots, ALL),
            home,
        ],
        Compute(
            functools.partial(forward_body, home),
            [qkv_got, info_got],
            [
                slot_type,
                jax.ShapeDtypeStruct(slot_type.shape, f32),
                jax.ShapeDtypeStruct((reps, 8, rows), f32),
            ],
            [
                pltpu.VMEM((rows, rows), f32),
                pltpu.VMEM((slots, HEAD_DIM, rows), f32),
                pltpu.VMEM((8, rows), f32),
            ],
        ),
    )
    attn_out_t = att_home.reshape(padded_heads * HEAD_DIM, rows)
    out_rows = out_full.reshape(shards, padded, width)
    down = down_full.reshape(ff_half, width)
    grad_out = got_grad.reshape(rows, width)
    late = ChunkGather(sizes, late_z)
    parts_type = jax.ShapeDtypeStruct((2, 2, rows, width), bf16)
    own_type = jax.ShapeDtypeStruct((rows, width), bf16)
    _, _, _, parts_got, gate_up_grad, down_grad, _, attn_branch = run(
        4,
        "feed_forward",
        sizes,
        [
            Swap(sizes, own_type).at(0, 1),
            Swap(sizes, own_type).at(0, 1),
            late,
            AllToAll(sizes, parts_type, ("core",), late=True, source=2).at(2),
        ],
        Compute(
            functools.partial(ffn_body, late),
            [
                first_full,
                down,
                attn_out_t,
                out_rows,
                hidden,
                grad_out,
                branch_scale,
                gain_two[None],
            ],
            [
                jax.ShapeDtypeStruct((shards, padded, 2 * ff_half), bf16),
                jax.ShapeDtypeStruct(down.shape, bf16),
                parts_type,
                jax.ShapeDtypeStruct((rows, width), f32),
            ],
            [
                pltpu.VMEM((shards, chips, chip_unit, 2 * FF_CHUNK), bf16),
                pltpu.VMEM((width, 2 * FF_CHUNK), bf16),
                pltpu.VMEM((2 * rows, width), f32),
                pltpu.VMEM((2 * rows, width), f32),
                pltpu.SemaphoreType.DMA((1,)),
            ],
        ),
        vmem=67_000_000,
    )
    parts = 2 if chips == 4 else 1
    out_grad_type = jax.ShapeDtypeStruct((shards, chips, 2, parts, rep_unit // parts, width), bf16)
    grad_got, _, result, base, vector_grads, out_grad = run(
        6,
        "grads",
        sizes,
        [AllToAll(sizes, slot_type, REP, late=True, source=0).at(0)],
        Compute(
            grads_body,
            [
                parts_got,
                hidden,
                attn_branch,
                grad_out,
                branch_scale,
                logit_scale,
                gain_two[None],
                full_router[None],
                out_rows,
                attn_out_t,
            ],
            [
                slot_type,
                tokens_type,
                jax.ShapeDtypeStruct((rows, width), f32),
                jax.ShapeDtypeStruct((8, width), f32),
                out_grad_type,
            ],
            [pltpu.VMEM((rows, width), bf16)],
        ),
    )
    gate_up_grad = gate_up_grad.reshape(shards, chips, parts, chip_unit // parts, 2 * ff_half)
    down_grad = down_grad.reshape(shards // 2, chips, parts, down_unit // parts, width)
    gate_up_sum, down_sum, out_sum, home_out, heads_home, _ = run(
        7,
        "attend_back",
        sizes,
        [
            Reduce(sizes, gate_up_grad, ("plane", "shard")).at(0, 2),
            Reduce(sizes, down_grad, ("plane",)).at(1),
            Reduce(sizes, out_grad, ("pair", "plane")).at(1),
            AllToAll(sizes, result, ALL),
            Heads(sizes, heads_type, False, 0),
        ],
        Compute(
            backward_body,
            [qkv_got, grad_got, att_keep, lse, info_got],
            [heads_type],
            [
                pltpu.VMEM((rows, rows), f32),
                pltpu.VMEM((reps, slots, HEAD_DIM, rows), f32),
                pltpu.VMEM((reps, slots, rows, HEAD_DIM), bf16),
                pltpu.VMEM((reps, slots, rows, HEAD_DIM), bf16),
                pltpu.VMEM((reps, 8, rows), f32),
            ],
        ),
    )

    qkv_columns = qkv_weights.shape[1]
    qkv_grad_type = jax.ShapeDtypeStruct(
        (shards, chips, 2, parts, rep_unit // parts, qkv_columns), bf16
    )
    vectors_type = jax.ShapeDtypeStruct((shards, 8, shard_rows), f32)
    qkv_home, gate_up_home, down_home, out_home, home_grad, vectors_home = run(
        8,
        "project_back",
        sizes,
        [
            Reduce(sizes, qkv_grad_type, ("pair", "plane", "shard", "spread"), late=True, source=1),
            Reduce(sizes, gate_up_sum, ("spread",)),
            Reduce(sizes, down_sum, ("shard", "spread"), half=True),
            Reduce(sizes, out_sum, ("shard", "spread")),
            AllToAll(sizes, tokens_type, ALL, late=True, source=0).at(0),
            AllToAll(sizes, vectors_type, ALL, by_shard=True, late=True, source=2).at(0),
        ],
        Compute(
            project_back_body,
            [
                heads_home,
                cosines,
                sines,
                qkv_weights,
                hidden,
                first_normalized,
                gain_one[None],
                base,
                vector_grads,
            ],
            [tokens_type, qkv_grad_type, vectors_type],
            [pltpu.VMEM((qkv_columns, rows), bf16)],
        ),
    )[:6]
    weight_grads = finalize(
        gate_up_home.reshape(chips, 2, chip_unit, 2 * ff_half),
        down_home.reshape(chips, down_unit, width),
        out_home.reshape(chips, chip_unit, width),
        qkv_home.reshape(chips, chip_unit, qkv_columns),
        slot_of_row,
        home_out.reshape(rows, width),
        home_grad.reshape(rows, width),
        shard_rows,
        key_matrix.shape[1],
    )
    gate_total, up_total, down_total, out_total, query_total, key_total, value_total = weight_grads[:7]
    vector_total = jnp.sum(vectors_home, axis=0)

    return (
        *weight_grads[7:],
        query_total,
        key_total,
        value_total,
        out_total,
        gate_total,
        up_total,
        down_total,
        vector_total[0],
        vector_total[1],
        vector_total[2],
    )


def solution(mesh):
    reps, shards = mesh.shape["rep"], mesh.shape["shard"]
    sizes = {"chip": reps // 2, "core": 2, "shard": shards}
    split_mesh = Mesh(mesh.devices.reshape(reps // 2, 2, shards), ALL)
    tokens, tokens_1d = P(ALL, None), P(ALL)
    weight, vector = P("shard", None), P("shard")
    return jax.shard_map(
        functools.partial(local, sizes),
        mesh=split_mesh,
        in_specs=(tokens, tokens, tokens_1d, weight, tokens_1d) + (weight,) * 7 + (vector,) * 3,
        out_specs=(tokens, tokens) + (weight,) * 7 + (vector,) * 3,
        check_vma=False,
    )
```

profile of v0, /device:TPU:0, one launch (start us, length us, event | category | flops | bytes accessed | tf_op | source)
XLA Modules:
  0.0 513.8 jit_solution(1904472866769751638)
XLA Ops:
  0.6 0.7 add_select_fusion
  1.9 0.6 pad.22.refs_1_
  2.5 2.0 convolution_convert_fusion
  4.5 1.3 copy.69
  5.8 0.9 fusion.refs_4_
  7.5 1.0 pad.25
  8.5 1.3 copy.73.refs_5_
  10.5 50.4 %first.1 = (bf16[32,16,960]{2,1,0:T(8,128)(2,1)}, s32[32,1,128]{2,1,0:T(1,128)}, f32[4,8,240]{2,1,0:T(8,128)}, bf16[4,8,32,1600]{3,2,1,0:T(8,128)(2,1)}, bf16[32...) custom-call(bf16[32,16,960]{2,1,0:T(8,128)(2,1)} %bitcast.43, ...), custom_call_target="tpu_custom_call" | custom-call | tf_op jit(solution)/shard_map/first/pallas_call | solution.py:877
  60.8 0.8 fusion.13
  62.9 0.7 and_select_fusion
  63.6 0.6 pad.27.refs_3_
  64.2 1.0 multiply_sine_fusion
  65.2 0.8 slice_bitcast_fusion
  66.0 0.7 slice.41.refs_6_.refs_9_
  66.7 0.8 pad.26
  67.5 46.1 %project.1 = (bf16[4,4,64,512]{3,2,1,0:T(8,128)(2,1)}, bf16[4,4,4,64,512]{4,3,2,1,0:T(8,128)(2,1)}, bf16[4,8,32,960]{3,2,1,0:T(8,128)(2,1)}, s32[8,8,512]{2,1,0:...) custom-call(bf16[4,64,512]{2,1,0:T(8,128)(2,1)} %get-tuple-element.6, ...), custom_call_target="tpu_custom_call" | custom-call | tf_op jit(solution)/shard_map/project/pallas_call | solution.py:877
  113.7 71.4 %attend.1 = (bf16[4,4,64,512]{3,2,1,0:T(8,128)(2,1)}, bf16[2,4,160,960]{3,2,1,0:T(8,128)(2,1)}, bf16[4,8,32,960]{3,2,1,0:T(8,128)(2,1)}, bf16[32,16,960]{2,1,0:T...) custom-call(bf16[4,4,64,512]{3,2,1,0:T(8,128)(2,1)} %get-tuple-eleme, ...), custom_call_target="tpu_custom_call", output_to_operand_aliasing={{0}: (0, {}), {2}: (2, {})} | custom-call | tf_op jit(solution)/shard_map/attend/pallas_call | solution.py:877
  185.7 0.7 compare_reduce_fusion
  186.6 0.9 subtract_multiply_fusion
  187.5 0.7 slice.44.refs_8_.refs_6_
  188.2 74.3 %feed_forward.1 = (bf16[2,512,960]{2,1,0:T(8,128)(2,1)}, bf16[2,512,960]{2,1,0:T(8,128)(2,1)}, bf16[4,4,4,64,512]{4,3,2,1,0:T(8,128)(2,1)}, bf16[2,2,512,960]{3,...) custom-call(bf16[4,4,4,64,512]{4,3,2,1,0:T(8,128)(2,1)} %get-tuple-e, ...), custom_call_target="tpu_custom_call", output_to_operand_aliasing={{2}: (0, {})} | custom-call | tf_op jit(solution)/shard_map/feed_forward/pallas_call | solution.py:877
  262.5 0.7 slice.45.refs_7_
  263.2 27.5 %grads.1 = (bf16[8,2,64,512]{3,2,1,0:T(8,128)(2,1)}, bf16[8,2,64,512]{3,2,1,0:T(8,128)(2,1)}, bf16[32,16,960]{2,1,0:T(8,128)(2,1)}, f32[512,960]{1,0:T(8,128)}, ...) custom-call(bf16[2,2,512,960]{3,2,1,0:T(8,128)(2,1)} %get-tuple-element.83.refs_0_, bf16[512,960]{1,0:T(8,128)(2,1)} %bitcast.34, ...), custom_call_target="tpu_custom_call" | custom-call | tf_op jit(solution)/shard_map/grads/pallas_call | solution.py:877
  290.7 120.0 %attend_back.1 = (bf16[2,32,2560]{2,1,0:T(8,128)(2,1)}, bf16[2,2,80,960]{3,2,1,0:T(8,128)(2,1)}, bf16[4,2,16,960]{3,2,1,0:T(8,128)(2,1)}, bf16[32,16,960]{2,1,0:...) custom-call(bf16[4,4,2,32,2560]{4,3,2,1,0:T(8,128)(2,1)} %bitcast.38, ...), custom_call_target="tpu_custom_call" | custom-call | tf_op jit(solution)/shard_map/attend_back/pallas_call | solution.py:877
  410.8 85.0 %project_back.1 = (bf16[4,2,2,16,1600]{4,3,2,1,0:T(8,128)(2,1)}, bf16[4,2,2,32,2560]{4,3,2,1,0:T(8,128)(2,1)}, bf16[4,2,80,960]{3,2,1,0:T(8,128)(2,1)}, bf16[4,2...) custom-call(bf16[2,32,2560]{2,1,0:T(8,128)(2,1)} %get-tuple-element., ...), custom_call_target="tpu_custom_call" | custom-call | tf_op jit(solution)/shard_map/project_back/pallas_call | solution.py:877
  495.8 0.9 copy.79.refs_4_
  496.7 8.8 %finalize.1 = (f32[240,2560]{1,0:T(8,128)}, f32[240,2560]{1,0:T(8,128)}, f32[640,960]{1,0:T(8,128)}, f32[240,960]{1,0:T(8,128)}, f32[240,960]{1,0:T(8,128)}, /*i...) custom-call(bf16[4,2,64,2560]{3,2,1,0:T(8,128)(2,1)} %bitcast.47, ...), custom_call_target="tpu_custom_call" | custom-call | tf_op jit(solution)/shard_map/finalize/pallas_call | solution.py:1375
  505.5 3.3 copy.84
  508.9 1.3 copy.80
  510.2 1.3 copy.81
  511.4 0.9 copy.82
  512.3 0.9 copy.83
  (64 shorter events, 4.6 us)
Async XLA Ops:
  2.5 4.3 copy-start.9
  2.5 4.4 copy-start.10
  2.5 4.6 copy-start.5
  5.8 2.7 copy-start.3
  7.1 2.7 copy-start.13
  7.1 2.7 copy-start.14
  7.1 2.7 copy-start.15
  10.5 51.2 %copy-start.16 = (s32[1,8]{1,0:T(1,128)S(1)}, s32[1,8]{1,0:T(1,128)}, u32[]{:S(2)}) copy-start(s32[1,8]{1,0:T(1,128)} %param.18) | copy-start | bytes 100
  10.5 51.5 %copy-start.12 = (s32[512]{0:T(512)S(1)}, s32[512]{0:T(512)}, u32[]{:S(2)}) copy-start(s32[512]{0:T(512)} %param.19) | copy-start | bytes 6148
  10.5 56.2 %copy-start.4 = (bf16[240,960]{1,0:T(8,128)(2,1)S(1)}, bf16[240,960]{1,0:T(8,128)(2,1)}, u32[]{:S(2)}) copy-start(bf16[240,960]{1,0:T(8,128)(2,1)} %param.23) | copy-start | bytes 1382404
  113.7 71.5 %copy-start = (bf16[32,16,960]{2,1,0:T(8,128)(2,1)S(1)}, bf16[32,16,960]{2,1,0:T(8,128)(2,1)}, u32[]{:S(2)}) copy-start(bf16[32,16,960]{2,1,0:T(8,128)(2,1)} %get-tuple-element.66) | copy-start | bytes 2949124
  113.7 72.0 %copy-start.11 = (s32[32,1,128]{2,1,0:T(1,128)S(1)}, s32[32,1,128]{2,1,0:T(1,128)}, u32[]{:S(2)}) copy-start(s32[32,1,128]{2,1,0:T(1,128)} %get-tuple-element.65) | copy-start | bytes 49156
  505.5 3.3 copy-start.2
  505.5 4.6 copy-start.1
  508.8 2.6 copy-start.7
  508.8 3.5 copy-start.6
  508.9 4.4 copy-start.8
where the time goes:
time: 514 us
  Pallas kernels  484 us (94%)
  local copies, waits for them, and re-layouts  20.4 us (4%)
  other arithmetic  6.83 us (1%)
    pallas_call x7, Pallas kernels, run(): pl.pallas_call(kernel, out_shape=out_shapes, in_specs=in_specs, out_specs...  475 us

commit v1 on v0

--- a/solution.py
+++ b/solution.py
@@ -765,7 +765,11 @@
             sent.append(lambda: shard_each(lambda copy: copy.wait_send()))
         if last == "spread":
             if "shard" not in self.stages:
-                mine[...] = now[...]
+
+                def keep():
+                    mine[...] = now[...]
+
+                guard(0, keep)
             self.plane.bind(
                 lambda t, c, k: out.at[c, t] if self.half else out.at[c, k, t],
                 lambda t: lax.rem(t, 2),
@@ -979,7 +983,7 @@
 
     @pl.loop(0, blocks)
     def _(j):
-        for n, step in enumerate((blocks // 2 - 1, blocks // 2, blocks - 2)):
+        for n, step in enumerate((blocks // 2, blocks // 2 + 1, blocks - 1)):
             pl.when(j == step)(lambda: hook(n))
         bias[...] = diagonal_bias(info_ref[j])
         mask = mask_rows(info_ref[j, 0:1])
@@ -1254,7 +1258,7 @@
     to_slot_ref, cotangent_ref, gate_ref, up_ref, down_ref = ins
     slots_ref, first_ref, late_ref, down_rows_ref = outs
     hook(0)
-    sent = dot(to_slot_ref[...], cotangent_ref[...]).astype(bf16)
+    sent = dot(to_slot_ref[...], cotangent_ref[...], 1, 1).astype(bf16)
     slots_ref[...] = sent.reshape(slots_ref.shape)
     chips, unit = first_ref.shape[:2]
     filled, half = gate_ref.shape[0], gate_ref.shape[1] // 2
@@ -1334,13 +1338,22 @@
 
 
 def finalize_kernel(*refs):
-    gate_up_ref, down_ref, out_ref, qkv_ref, slot_ref, result_ref, grad_ref = refs[:7]
-    gate, up, down, out, query, key, value, result, grad = refs[7:]
-    lanes = lax.broadcasted_iota(jnp.int32, (slot_ref.shape[0], result_ref.shape[0]), 1)
-    from_slot = jnp.where(lanes == slot_ref[...], 1.0, 0.0).astype(bf16)
-    result[...] = dot(from_slot, result_ref[...]).astype(bf16)
-    grad[...] = dot(from_slot, grad_ref[...]).astype(bf16)
+    gate_up_ref, out_ref, down_ref, qkv_ref, slot_ref, result_ref, grad_ref = refs[:7]
+    gate, up, out, query, down, key, value, result, grad = refs[7:]
     cores, rows, columns = gate_up_ref.shape[1:]
+    query_end = query.shape[1]
+
+    @pl.when(pl.program_id(0) == 0)
+    def _():
+        slots = lax.broadcasted_iota(jnp.int32, (result_ref.shape[0], slot_ref.shape[1]), 0)
+        to_slot = jnp.where(slots == slot_ref[...], 1.0, 0.0).astype(bf16)
+        result[...] = dot(result_ref[...], to_slot, 0, 0).astype(bf16)
+        grad[...] = dot(grad_ref[...], to_slot, 0, 0).astype(bf16)
+        down[...] = jnp.transpose(down_ref[...]).astype(f32)
+        heads = jnp.transpose(qkv_ref[:, query_end:])[:, : key.shape[1]].astype(f32)
+        key[...] = heads[: key.shape[0]]
+        value[...] = heads[key.shape[0] :]
+
     half = columns // 2
     for core in range(cores):
         for start in range(0, columns, 2 * FF_CHUNK):
@@ -1348,42 +1361,37 @@
             middle = start + FF_CHUNK
             gate[:, at : at + FF_CHUNK] = gate_up_ref[0, core, :, start:middle].astype(f32)
             up[:, at : at + FF_CHUNK] = gate_up_ref[0, core, :, middle : middle + FF_CHUNK].astype(f32)
-    down[...] = down_ref[0].astype(f32)
     out[...] = out_ref[0].astype(f32)
-    ends = (query.shape[1], query.shape[1] + key.shape[1])
-    qkv = qkv_ref[0].astype(f32)
-    query[...] = qkv[:, : ends[0]]
-    key[...] = qkv[:, ends[0] : ends[1]]
-    value[...] = qkv[:, ends[1] :]
-
-
-def finalize(gate_up, down, out, qkv, slot_of_row, result, grad, shard_rows, key_width):
+    at = pl.ds(pl.multiple_of(pl.program_id(0) * rows, rows), rows)
+    query[...] = qkv_ref[at, :query_end].astype(f32)
+
+
+def finalize(gate_up, out, down, qkv, slot_of_row, result, grad, shard_rows, key_width):
     chips, rows = gate_up.shape[0], gate_up.shape[2]
     width, hidden = out.shape[2], gate_up.shape[3]
-    columns = (hidden, hidden, None, width, width, key_width, key_width)
-    count = result.shape[0] // chips
-
-    def out_spec(array_columns):
-        shape = tuple(down.shape[1:]) if array_columns is None else (rows, array_columns)
-        return pl.BlockSpec(shape, lambda c: (c, 0))
-
-    def out_type(array_columns):
-        shape = (chips * down.shape[1], down.shape[2])
-        shape = shape if array_columns is None else (shard_rows, array_columns)
-        return jax.ShapeDtypeStruct(shape, f32)
-
-    return pl.pallas_call(
+    by_chip = [(shard_rows, hidden), (shard_rows, hidden), (shard_rows, width), (shard_rows, width)]
+    whole = [((width, down.shape[0]), f32)] + [((key_width, shard_rows), f32)] * 2
+    whole += [((width, result.shape[0]), bf16)] * 2
+
+    def full(shape):
+        return pl.BlockSpec(tuple(shape), lambda c: (0,) * len(shape))
+
+    slots = slot_of_row[None]
+    totals = pl.pallas_call(
         finalize_kernel,
         grid=(chips,),
-        in_specs=[pl.BlockSpec((1, 2, rows, hidden), lambda c: (c, 0, 0, 0))]
-        + [pl.BlockSpec((1,) + tuple(a.shape[1:]), lambda c: (c, 0, 0)) for a in (down, out, qkv)]
-        + [pl.BlockSpec((count, 1), lambda c: (c, 0))]
-        + [pl.BlockSpec(result.shape, lambda c: (0, 0))] * 2,
-        out_specs=[out_spec(c) for c in columns]
-        + [pl.BlockSpec((count, width), lambda c: (c, 0))] * 2,
-        out_shape=[out_type(c) for c in columns] + [jax.ShapeDtypeStruct(result.shape, bf16)] * 2,
+        in_specs=[
+            pl.BlockSpec((1, 2, rows, hidden), lambda c: (c, 0, 0, 0)),
+            pl.BlockSpec((1, rows, width), lambda c: (c, 0, 0)),
+        ]
+        + [full(array.shape) for array in (down, qkv, slots, result, grad)],
+        out_specs=[pl.BlockSpec((rows, shape[1]), lambda c: (c, 0)) for shape in by_chip]
+        + [full(shape) for shape, _ in whole],
+        out_shape=[jax.ShapeDtypeStruct(shape, f32) for shape in by_chip]
+        + [jax.ShapeDtypeStruct(shape, dtype) for shape, dtype in whole],
         name="finalize",
-    )(gate_up, down, out, qkv, slot_of_row[:, None], result, grad)
+    )(gate_up, out, down, qkv, slots, result, grad)
+    return list(totals[:4]) + [jnp.transpose(total) for total in totals[4:]]
 
 
 def rounded_up(value, unit):
@@ -1463,7 +1471,13 @@
         ],
         Compute(
             prepare_body,
-            [to_slot_b, cotangent, gate_weight, up_weight, jnp.transpose(down_weight)],
+            [
+                to_slot_b,
+                jnp.transpose(cotangent),
+                gate_weight,
+                up_weight,
+                jnp.transpose(down_weight),
+            ],
             [
                 tokens_type,
                 first_type,
@@ -1684,22 +1698,22 @@
             [pltpu.VMEM((qkv_columns, rows), bf16)],
         ),
     )[:6]
-    weight_grads = finalize(
+    totals = finalize(
         gate_up_home.reshape(chips, 2, chip_unit, 2 * ff_half),
-        down_home.reshape(chips, down_unit, width),
         out_home.reshape(chips, chip_unit, width),
-        qkv_home.reshape(chips, chip_unit, qkv_columns),
+        down_home.reshape(chips * down_unit, width),
+        qkv_home.reshape(padded, qkv_columns),
         slot_of_row,
         home_out.reshape(rows, width),
         home_grad.reshape(rows, width),
         shard_rows,
         key_matrix.shape[1],
     )
-    gate_total, up_total, down_total, out_total, query_total, key_total, value_total = weight_grads[:7]
+    gate_total, up_total, out_total, query_total, down_total, key_total, value_total = totals[:7]
     vector_total = jnp.sum(vectors_home, axis=0)
 
     return (
-        *weight_grads[7:],
+        *totals[7:],
         query_total,
         key_total,
         value_total,

time: 514 us -> 512 us (level)
  local copies, waits for them, and re-layouts: 20.4 us -> 15.2 us
    unnamed x42 -> x10, local copies, waits for them, and re-layouts: 9.32 us -> 2.16 us
where the time goes in v1:
time: 512 us; the launch traced here: 511 us
  Pallas kernels  484 us (95%)
  local copies, waits for them, and re-layouts  15.2 us (3%)
  other arithmetic  10.4 us (2%)
    pallas_call x7, Pallas kernels, run(): pl.pallas_call(kernel, out_shape=out_shapes, in_specs=in_specs, out_specs...  475 us

profile of v1, /device:TPU:0, one launch (start us, length us, event | category | flops | bytes accessed | tf_op | source)
XLA Modules:
  0.0 511.3 jit_solution(814747159037460196)
XLA Ops:
  0.7 0.9 reduce-window.4
  2.1 0.7 stack.17
  2.8 0.7 stack.18
  3.5 0.7 stack.19
  4.1 0.7 add_select_fusion
  6.6 1.1 copy.51
  7.7 1.1 copy.52
  8.7 1.3 concatenate.3
  10.1 1.0 pad.25
  11.0 0.9 fusion.refs_4_
  12.0 0.8 pad.26
  12.8 0.7 convolution_convert_fusion
  13.6 1.3 copy.49
  14.9 50.3 %first.1 = (bf16[32,16,960]{2,1,0:T(8,128)(2,1)}, s32[32,1,128]{2,1,0:T(1,128)}, f32[4,8,240]{2,1,0:T(8,128)}, bf16[4,8,32,1600]{3,2,1,0:T(8,128)(2,1)}, bf16[32...) custom-call(bf16[32,16,960]{2,1,0:T(8,128)(2,1)} %bitcast.49, ...), custom_call_target="tpu_custom_call" | custom-call | tf_op jit(solution)/shard_map/first/pallas_call | solution.py:881
  65.2 1.4 compare_reduce_fusion
  66.6 0.8 slice_bitcast_fusion
  67.4 0.7 slice.44.refs_8_.refs_6_
  68.1 0.7 slice.41.refs_6_.refs_9_
  68.8 0.7 slice.45.refs_7_
  69.5 1.5 multiply_reduce_fusion
  71.1 0.8 fusion.13
  72.4 0.7 and_select_fusion
  73.9 1.0 multiply_sine_fusion
  75.0 0.9 subtract_multiply_fusion
  75.9 46.1 %project.1 = (bf16[4,4,64,512]{3,2,1,0:T(8,128)(2,1)}, bf16[4,4,4,64,512]{4,3,2,1,0:T(8,128)(2,1)}, bf16[4,8,32,960]{3,2,1,0:T(8,128)(2,1)}, s32[8,8,512]{2,1,0:...) custom-call(bf16[4,64,512]{2,1,0:T(8,128)(2,1)} %get-tuple-element.6, ...), custom_call_target="tpu_custom_call" | custom-call | tf_op jit(solution)/shard_map/project/pallas_call | solution.py:881
  122.1 71.3 %attend.1 = (bf16[4,4,64,512]{3,2,1,0:T(8,128)(2,1)}, bf16[2,4,160,960]{3,2,1,0:T(8,128)(2,1)}, bf16[4,8,32,960]{3,2,1,0:T(8,128)(2,1)}, bf16[32,16,960]{2,1,0:T...) custom-call(bf16[4,4,64,512]{3,2,1,0:T(8,128)(2,1)} %get-tuple-eleme, ...), custom_call_target="tpu_custom_call", output_to_operand_aliasing={{0}: (0, {}), {2}: (2, {})} | custom-call | tf_op jit(solution)/shard_map/attend/pallas_call | solution.py:881
  193.4 74.3 %feed_forward.1 = (bf16[2,512,960]{2,1,0:T(8,128)(2,1)}, bf16[2,512,960]{2,1,0:T(8,128)(2,1)}, bf16[4,4,4,64,512]{4,3,2,1,0:T(8,128)(2,1)}, bf16[2,2,512,960]{3,...) custom-call(bf16[4,4,4,64,512]{4,3,2,1,0:T(8,128)(2,1)} %get-tuple-e, ...), custom_call_target="tpu_custom_call", output_to_operand_aliasing={{2}: (0, {})} | custom-call | tf_op jit(solution)/shard_map/feed_forward/pallas_call | solution.py:881
  267.8 27.3 %grads.1 = (bf16[8,2,64,512]{3,2,1,0:T(8,128)(2,1)}, bf16[8,2,64,512]{3,2,1,0:T(8,128)(2,1)}, bf16[32,16,960]{2,1,0:T(8,128)(2,1)}, f32[512,960]{1,0:T(8,128)}, ...) custom-call(bf16[2,2,512,960]{3,2,1,0:T(8,128)(2,1)} %get-tuple-element.83.refs_0_, bf16[512,960]{1,0:T(8,128)(2,1)} %bitcast.40, ...), custom_call_target="tpu_custom_call" | custom-call | tf_op jit(solution)/shard_map/grads/pallas_call | solution.py:881
  295.1 120.0 %attend_back.1 = (bf16[2,32,2560]{2,1,0:T(8,128)(2,1)}, bf16[2,2,80,960]{3,2,1,0:T(8,128)(2,1)}, bf16[4,2,16,960]{3,2,1,0:T(8,128)(2,1)}, bf16[32,16,960]{2,1,0:...) custom-call(bf16[4,4,2,32,2560]{4,3,2,1,0:T(8,128)(2,1)} %bitcast.44, ...), custom_call_target="tpu_custom_call" | custom-call | tf_op jit(solution)/shard_map/attend_back/pallas_call | solution.py:881
  415.1 85.1 %project_back.1 = (bf16[4,2,2,16,1600]{4,3,2,1,0:T(8,128)(2,1)}, bf16[4,2,2,32,2560]{4,3,2,1,0:T(8,128)(2,1)}, bf16[4,2,80,960]{3,2,1,0:T(8,128)(2,1)}, bf16[4,2...) custom-call(bf16[2,32,2560]{2,1,0:T(8,128)(2,1)} %get-tuple-element., ...), custom_call_target="tpu_custom_call" | custom-call | tf_op jit(solution)/shard_map/project_back/pallas_call | solution.py:881
  500.2 1.0 reduce_sum.62
  501.8 9.3 %finalize.1 = (f32[240,2560]{1,0:T(8,128)}, f32[240,2560]{1,0:T(8,128)}, f32[240,960]{1,0:T(8,128)}, f32[240,960]{1,0:T(8,128)}, f32[960,640]{1,0:T(8,128)}, /*i...) custom-call(bf16[4,2,64,2560]{3,2,1,0:T(8,128)(2,1)} %bitcast.52, ...), custom_call_target="tpu_custom_call" | custom-call | tf_op jit(solution)/shard_map/finalize/pallas_call | solution.py:1380
  (31 shorter events, 4.6 us)
Async XLA Ops:
  0.6 11.3 %copy-start = (bf16[240,960]{1,0:T(8,128)(2,1)S(1)}, bf16[240,960]{1,0:T(8,128)(2,1)}, u32[]{:S(2)}) copy-start(bf16[240,960]{1,0:T(8,128)(2,1)} %param.23) | copy-start | bytes 1382404
  5.1 7.7 %copy-start.1 = (s32[512]{0:T(512)}, s32[512]{0:T(512)S(1)}, u32[]{:S(2)}) copy-start(s32[512]{0:T(512)S(1)} %multiply_add_fusion) | copy-start | bytes 6148
  8.7 4.1 copy-start.3
  14.9 57.3 %copy-start.2 = (s32[512]{0:T(512)S(1)}, s32[512]{0:T(512)}, u32[]{:S(2)}) copy-start(s32[512]{0:T(512)} %param.19) | copy-start | bytes 6148

commit v2 on v1

--- a/solution.py
+++ b/solution.py
@@ -207,35 +207,41 @@
         self.out_shapes = [jax.ShapeDtypeStruct(array.shape, array.dtype)]
         self.out_specs = [VMEM_SPEC]
         dma = pltpu.SemaphoreType.DMA
-        self.scratch = [dma((2, self.count)), dma((2, self.count))]
-
-    def copy(self, k, ins, outs, scratch, extra, sending):
+        self.scratch = [dma((3, self.count)), dma((3, self.count))]
+        self.bounds = (0, self.slots, self.main, self.units)
+
+    def copy(self, k, ins, outs, scratch, part, sending):
         me = lax.axis_index(REP)
         peer, coords = partner(k, REP, self.sizes, not sending)
-        units = pl.ds(self.main, self.units - self.main) if extra else pl.ds(0, self.main)
+        units = pl.ds(self.bounds[part], self.bounds[part + 1] - self.bounds[part])
         return peer, remote(
             ins[0].at[peer, units],
             outs[0].at[me if sending else peer, units],
-            scratch[0].at[int(extra), k],
-            scratch[1].at[int(extra), k],
+            scratch[0].at[part, k],
+            scratch[1].at[part, k],
             coords,
         )
 
-    def every(self, ins, outs, scratch, sending, act):
-        def main(k):
-            act(self.copy(k, ins, outs, scratch, False, sending)[1])
+    def every(self, ins, outs, scratch, sending, act, parts=(0, 1, 2)):
+        def main(k, part):
+            act(self.copy(k, ins, outs, scratch, part, sending)[1])
 
         def extra(k):
-            peer, copy = self.copy(k, ins, outs, scratch, True, sending)
+            peer, copy = self.copy(k, ins, outs, scratch, 2, sending)
             owner = peer if sending == self.to else lax.axis_index(REP)
             pl.when(apart(owner) == 1)(lambda: act(copy))
 
-        each(1, self.count, main)
-        if self.units > self.main:
-            each(1, self.count, extra)
+        for part in parts:
+            if part < 2:
+                each(1, self.count, lambda k: main(k, part))
+            elif self.units > self.main:
+                each(1, self.count, extra)
 
     def steps(self, ins, outs, scratch):
-        self.every(ins, outs, scratch, True, lambda copy: copy.start())
+        self.every(ins, outs, scratch, True, lambda copy: copy.start(), (0,))
+        if self.hooks:
+            yield
+        self.every(ins, outs, scratch, True, lambda copy: copy.start(), (1, 2))
         me = lax.axis_index(REP)
         outs[0][me] = ins[0][me]
         yield
@@ -1164,6 +1170,9 @@
         unit = (slot, key_unit(slots, slot), value_unit(slots, slot))[kind]
         sent_ref[head // slots, unit] = value
 
+    for head in range(QUERY_HEADS, reps * slots):
+        for kind in range(3):
+            put(kind, head, jnp.zeros((HEAD_DIM, rows), bf16))
     for start in range(0, columns, 256):
         stop = min(start + 256, columns)
         block = jnp.transpose(dot(normed, full_ref[:, start:stop]))
@@ -1192,9 +1201,9 @@
                 value = block[at : at + HEAD_DIM].astype(bf16)
                 for m in range(GROUP):
                     put(2, (head - QUERY_HEADS - KEY_VALUE_HEADS) * GROUP + m, value)
-    for head in range(QUERY_HEADS, reps * slots):
-        for kind in range(3):
-            put(kind, head, jnp.zeros((HEAD_DIM, rows), bf16))
+        if start < QUERY_HEADS * HEAD_DIM <= stop:
+            hook(0)
+    hook(1)
 
 
 def project_back_body(ins, outs, tmp, hook):
@@ -1521,7 +1530,7 @@
             Gather(sizes, late_shard, ("chip",), "z"),
             Gather(sizes, out_shard, REP, "z"),
             AllToAll(sizes, info, REP, spread=True),
-            Heads(sizes, heads_type, True, 0),
+            Heads(sizes, heads_type, True, 0).at(0, 1),
         ],
         Compute(
             project_body,

time: 512 us -> 512 us (level)
  no operation moved by 1% of the time
where the time goes in v2:
time: 512 us
  Pallas kernels  484 us (95%)
  local copies, waits for them, and re-layouts  15.2 us (3%)
  other arithmetic  10.4 us (2%)
    pallas_call x7, Pallas kernels, run(): pl.pallas_call(kernel, out_shape=out_shapes, in_specs=in_specs, out_specs...  475 us

profile of v2, /device:TPU:0, one launch (start us, length us, event | category | flops | bytes accessed | tf_op | source)
XLA Modules:
  0.0 511.8 jit_solution(15275978564517984651)
XLA Ops:
  0.7 0.9 reduce-window.4
  2.1 0.7 stack.17
  2.8 0.7 stack.18
  3.5 0.7 stack.19
  4.1 0.7 add_select_fusion
  6.6 1.1 copy.51
  7.7 1.1 copy.52
  8.7 1.3 concatenate.3
  10.1 1.0 pad.25
  11.0 0.9 fusion.refs_4_
  12.0 0.8 pad.26
  12.8 0.7 convolution_convert_fusion
  13.6 1.3 copy.49
  14.9 50.3 %first.1 = (bf16[32,16,960]{2,1,0:T(8,128)(2,1)}, s32[32,1,128]{2,1,0:T(1,128)}, f32[4,8,240]{2,1,0:T(8,128)}, bf16[4,8,32,1600]{3,2,1,0:T(8,128)(2,1)}, bf16[32...) custom-call(bf16[32,16,960]{2,1,0:T(8,128)(2,1)} %bitcast.49, ...), custom_call_target="tpu_custom_call" | custom-call | tf_op jit(solution)/shard_map/first/pallas_call | solution.py:887
  65.2 1.4 compare_reduce_fusion
  66.6 0.8 slice_bitcast_fusion
  67.4 0.7 slice.44.refs_8_.refs_6_
  68.1 0.7 slice.41.refs_6_.refs_9_
  68.8 0.7 slice.45.refs_7_
  69.5 1.5 multiply_reduce_fusion
  71.1 0.8 fusion.13
  72.4 0.7 and_select_fusion
  73.9 1.0 multiply_sine_fusion
  75.0 0.9 subtract_multiply_fusion
  75.9 46.4 %project.1 = (bf16[4,4,64,512]{3,2,1,0:T(8,128)(2,1)}, bf16[4,4,4,64,512]{4,3,2,1,0:T(8,128)(2,1)}, bf16[4,8,32,960]{3,2,1,0:T(8,128)(2,1)}, s32[8,8,512]{2,1,0:...) custom-call(bf16[4,64,512]{2,1,0:T(8,128)(2,1)} %get-tuple-element.6, ...), custom_call_target="tpu_custom_call" | custom-call | tf_op jit(solution)/shard_map/project/pallas_call | solution.py:887
  122.3 71.4 %attend.1 = (bf16[4,4,64,512]{3,2,1,0:T(8,128)(2,1)}, bf16[2,4,160,960]{3,2,1,0:T(8,128)(2,1)}, bf16[4,8,32,960]{3,2,1,0:T(8,128)(2,1)}, bf16[32,16,960]{2,1,0:T...) custom-call(bf16[4,4,64,512]{3,2,1,0:T(8,128)(2,1)} %get-tuple-eleme, ...), custom_call_target="tpu_custom_call", output_to_operand_aliasing={{0}: (0, {}), {2}: (2, {})} | custom-call | tf_op jit(solution)/shard_map/attend/pallas_call | solution.py:887
  193.7 74.3 %feed_forward.1 = (bf16[2,512,960]{2,1,0:T(8,128)(2,1)}, bf16[2,512,960]{2,1,0:T(8,128)(2,1)}, bf16[4,4,4,64,512]{4,3,2,1,0:T(8,128)(2,1)}, bf16[2,2,512,960]{3,...) custom-call(bf16[4,4,4,64,512]{4,3,2,1,0:T(8,128)(2,1)} %get-tuple-e, ...), custom_call_target="tpu_custom_call", output_to_operand_aliasing={{2}: (0, {})} | custom-call | tf_op jit(solution)/shard_map/feed_forward/pallas_call | solution.py:887
  268.0 27.3 %grads.1 = (bf16[8,2,64,512]{3,2,1,0:T(8,128)(2,1)}, bf16[8,2,64,512]{3,2,1,0:T(8,128)(2,1)}, bf16[32,16,960]{2,1,0:T(8,128)(2,1)}, f32[512,960]{1,0:T(8,128)}, ...) custom-call(bf16[2,2,512,960]{3,2,1,0:T(8,128)(2,1)} %get-tuple-element.83.refs_0_, bf16[512,960]{1,0:T(8,128)(2,1)} %bitcast.40, ...), custom_call_target="tpu_custom_call" | custom-call | tf_op jit(solution)/shard_map/grads/pallas_call | solution.py:887
  295.4 120.2 %attend_back.1 = (bf16[2,32,2560]{2,1,0:T(8,128)(2,1)}, bf16[2,2,80,960]{3,2,1,0:T(8,128)(2,1)}, bf16[4,2,16,960]{3,2,1,0:T(8,128)(2,1)}, bf16[32,16,960]{2,1,0:...) custom-call(bf16[4,4,2,32,2560]{4,3,2,1,0:T(8,128)(2,1)} %bitcast.44, ...), custom_call_target="tpu_custom_call" | custom-call | tf_op jit(solution)/shard_map/attend_back/pallas_call | solution.py:887
  415.6 85.1 %project_back.1 = (bf16[4,2,2,16,1600]{4,3,2,1,0:T(8,128)(2,1)}, bf16[4,2,2,32,2560]{4,3,2,1,0:T(8,128)(2,1)}, bf16[4,2,80,960]{3,2,1,0:T(8,128)(2,1)}, bf16[4,2...) custom-call(bf16[2,32,2560]{2,1,0:T(8,128)(2,1)} %get-tuple-element., ...), custom_call_target="tpu_custom_call" | custom-call | tf_op jit(solution)/shard_map/project_back/pallas_call | solution.py:887
  500.7 1.0 reduce_sum.62
  502.3 9.3 %finalize.1 = (f32[240,2560]{1,0:T(8,128)}, f32[240,2560]{1,0:T(8,128)}, f32[240,960]{1,0:T(8,128)}, f32[240,960]{1,0:T(8,128)}, f32[960,640]{1,0:T(8,128)}, /*i...) custom-call(bf16[4,2,64,2560]{3,2,1,0:T(8,128)(2,1)} %bitcast.52, ...), custom_call_target="tpu_custom_call" | custom-call | tf_op jit(solution)/shard_map/finalize/pallas_call | solution.py:1389
  (31 shorter events, 4.6 us)
Async XLA Ops:
  0.6 11.3 %copy-start = (bf16[240,960]{1,0:T(8,128)(2,1)S(1)}, bf16[240,960]{1,0:T(8,128)(2,1)}, u32[]{:S(2)}) copy-start(bf16[240,960]{1,0:T(8,128)(2,1)} %param.23) | copy-start | bytes 1382404
  5.1 7.7 %copy-start.1 = (s32[512]{0:T(512)}, s32[512]{0:T(512)S(1)}, u32[]{:S(2)}) copy-start(s32[512]{0:T(512)S(1)} %multiply_add_fusion) | copy-start | bytes 6148
  8.7 4.1 copy-start.3
  14.9 57.3 %copy-start.2 = (s32[512]{0:T(512)S(1)}, s32[512]{0:T(512)}, u32[]{:S(2)}) copy-start(s32[512]{0:T(512)} %param.19) | copy-start | bytes 6148
